TPU v7x, 256 devices: a whole 4x4x8 slice. The times are simulated.
256 devices in a mesh: wide: 64 (over x, y, z_lo, core), narrow: 4 (over z_hi).
Axes of the slice: x: 4, y: 4, z: 8 (z_hi: 4, z_lo: 2; z = z_hi * 2 + z_lo), core: 2. Of those that a mesh axis runs over, the one named last changes fastest.
Arguments:
- volume: bfloat16 [64, 128, 32, 512], P(None, 'wide', 'narrow'), may hold values from -6 to 6
- out_grad: bfloat16 [64, 128, 32, 512], P(None, 'wide', 'narrow'), may hold values from -6 to 6
- plane_kernel: bfloat16 [9, 64, 64], replicated, may hold values from -0.25 to 0.25
- z_axis_kernel: bfloat16 [7, 64, 64], replicated, may hold values from -0.25 to 0.25
Outputs:
- volume_grad: bfloat16 [64, 128, 32, 512], P(None, 'wide', 'narrow')
- plane_kernel_grad: float32 [9, 64, 64], replicated
- z_axis_kernel_gradient: float32 [7, 64, 64], replicated
All inputs are finite; a program needn't handle non-finite values.
Results may differ from a plain program's by a relative error of at most 0.0061.
Values may be sent and summed in bfloat16 or wider, within the bound.
No kernel may reach another device: no remote copies, remote signals or barrier semaphores. Data moves between devices by JAX's collectives and lax.ppermute only.
A program may use at most 192 MiB of HBM per device.

v0:
```python
import math

import jax
import jax.numpy as jnp
from jax import lax
from jax.sharding import Mesh
from jax.sharding import PartitionSpec as P

Z_DILATION = 4
WIDE = ("wide_0", "wide_1", "wide_2", "wide_3")
WIDE_NARROW = ("wide_0", "wide_1", "wide_2", "wide_3", "narrow")


def with_halo(block, sides, width):
    for axis, dim in sides:
        count = lax.axis_size(axis)
        forward = [(i, i + 1) for i in range(count - 1)]
        backward = [(target, source) for source, target in forward]
        low = lax.ppermute(
            lax.slice_in_dim(block, block.shape[dim] - width, None, axis=dim), axis, forward
        )
        high = lax.ppermute(lax.slice_in_dim(block, 0, width, axis=dim), axis, backward)
        block = jnp.concatenate([low, block, high], axis=dim)
    return block


def in_blocks(shard, dim, peers):
    lengths = shard.shape
    tiles = shard.reshape(*lengths[:dim], peers, lengths[dim] // peers, *lengths[dim + 1 :])
    return jnp.moveaxis(tiles, dim, 0)


def in_order(tiles, dim):
    tiles = jnp.moveaxis(tiles, 0, dim)
    lengths = tiles.shape
    return tiles.reshape(*lengths[:dim], lengths[dim] * lengths[dim + 1], *lengths[dim + 2 :])


def moved_by_axis(tiles, axes, sequence):
    lengths = [lax.axis_size(a) for a in axes]
    tiles = tiles.reshape(*lengths, *tiles.shape[1:])
    for k in sequence:
        tiles = lax.all_to_all(tiles, axes[k], split_axis=k, concat_axis=k, tiled=True)
    return tiles.reshape(-1, *tiles.shape[len(axes) :])


def two_step_exchange(shard, groups, sequence, split_dim, concat_dim):
    peers = lax.axis_size(groups[0]) * lax.axis_size(groups[1])
    tiles = in_blocks(shard, split_dim, peers)
    return in_order(moved_by_axis(tiles, groups, sequence), concat_dim)


def packed_total(arrays, axis):
    ravelled, at, finished = (jnp.concatenate([a.reshape(-1) for a in arrays]), 0, [])
    so_far = lax.psum(ravelled, axis)
    for a in arrays:
        finished.append(so_far[at : at + a.size].reshape(a.shape))
        at += a.size
    return tuple(finished)


def silu_slope(values):
    sigmoid = jax.nn.sigmoid(values)
    return sigmoid * (1.0 + values * (1.0 - sigmoid))


def plane_stack(rimmed, rows, cols, flipped):
    padded = jnp.pad(rimmed, ((0, 0), (0, 0), (0, 0), (1, 1)))
    pieces = []
    for kernel_tap_index in range(9):
        source_tap = 8 - kernel_tap_index if flipped else kernel_tap_index
        row_shift = source_tap // 3
        col_shift = source_tap % 3
        pieces.append(padded[:, :, row_shift : row_shift + rows, col_shift : col_shift + cols])
    return jnp.concatenate(pieces, axis=0)


def depth_stack(pencil, kernel_extent, flipped):
    depth_axis_size = pencil.shape[1]
    padded = jnp.pad(pencil, ((0, 0), (kernel_extent, kernel_extent), (0, 0)))
    pieces = []
    for kernel_tap_index in range(7):
        source_tap = 6 - kernel_tap_index if flipped else kernel_tap_index
        start = source_tap * Z_DILATION
        pieces.append(padded[:, start : start + depth_axis_size])
    return jnp.concatenate(pieces, axis=0)


def stacked_mixing(weight, stacked, out_shape):
    mixed = jnp.dot(
        weight, stacked.reshape(stacked.shape[0], -1), preferred_element_type=jnp.float32
    )
    return mixed.reshape(out_shape)


def stacked_kernel_grad(left, stacked, taps):
    width = left.shape[0]
    product = jnp.dot(
        left.reshape(width, -1),
        stacked.reshape(stacked.shape[0], -1).T,
        preferred_element_type=jnp.float32,
    )
    return product.reshape(width, taps, width).transpose(1, 0, 2)


def on_device(volume, out_grad, plane_kernel, z_axis_kernel):
    width, slabs, rows, cols = volume.shape
    cells = rows * cols
    kernel_extent = 3 * Z_DILATION
    plane_forward = plane_kernel.transpose(1, 0, 2).reshape(width, 9 * width)
    plane_backward = plane_kernel.transpose(2, 0, 1).reshape(width, 9 * width)
    depth_forward = z_axis_kernel.transpose(1, 0, 2).reshape(width, 7 * width)
    depth_backward = z_axis_kernel.transpose(2, 0, 1).reshape(width, 7 * width)
    grad_pencil = lax.all_to_all(
        out_grad.reshape(width, slabs, cells), WIDE, split_axis=2, concat_axis=1, tiled=True
    )
    rimmed = with_halo(volume, (("narrow", 2),), 1)
    volume_stack = plane_stack(rimmed, rows, cols, False)
    pre_act = stacked_mixing(plane_forward, volume_stack, volume.shape)
    acts = jax.nn.silu(pre_act).astype(jnp.bfloat16)
    act_slab = acts.reshape(width, slabs, cells)
    act_pencil = two_step_exchange(
        act_slab, (("wide_0", "wide_1", "wide_2"), "wide_3"), (1, 0), 2, 1
    )
    depth_axis_size = act_pencil.shape[1]
    act_stack = depth_stack(act_pencil, kernel_extent, False)
    depth_output = stacked_mixing(depth_forward, act_stack, act_pencil.shape)
    depth_gradient = (grad_pencil.astype(jnp.float32) * silu_slope(depth_output)).astype(
        jnp.bfloat16
    )
    depth_term = stacked_kernel_grad(depth_gradient, act_stack, 7)
    grad_stack = depth_stack(depth_gradient, kernel_extent, True)
    activation_gradient = stacked_mixing(depth_backward, grad_stack, act_pencil.shape).astype(
        jnp.bfloat16
    )
    slab_grad = lax.all_to_all(
        activation_gradient, WIDE, split_axis=1, concat_axis=2, tiled=True
    ).reshape(width, slabs, rows, cols)
    gradient_scale = 1.0 / math.sqrt(depth_axis_size * rows * lax.axis_size("narrow") * cols)
    pre_grad = (slab_grad.astype(jnp.float32) * silu_slope(pre_act)).astype(jnp.bfloat16)
    plane_term = stacked_kernel_grad(pre_grad, volume_stack, 9)
    grad_rimmed = with_halo(pre_grad, (("narrow", 2),), 1)
    pre_stack = plane_stack(grad_rimmed, rows, cols, True)
    volume_grad = out_grad.astype(jnp.float32) + stacked_mixing(
        plane_backward, pre_stack, volume.shape
    )
    plane_total, depth_total = packed_total((plane_term, depth_term), WIDE_NARROW)
    return (
        volume_grad.astype(jnp.bfloat16),
        plane_total * gradient_scale,
        depth_total * gradient_scale,
    )


def solution(mesh):
    finer = Mesh(
        mesh.devices.reshape(4, 4, 2, 2, mesh.shape["narrow"]),
        ("wide_0", "wide_1", "wide_2", "wide_3", "narrow"),
    )
    return jax.shard_map(
        on_device,
        mesh=finer,
        in_specs=(P(None, WIDE, "narrow", None), P(None, WIDE, "narrow", None), P(), P()),
        out_specs=(P(None, WIDE, "narrow", None), P(), P()),
        check_vma=False,
    )
```

profile of v0, /device:TPU:2, one launch (start us, length us, event | category | flops | bytes accessed | tf_op | source)
XLA Modules:
  0.0 652.0 jit_solution(14220006954756326169)
XLA Ops:
  11.3 6.4 collective-permute-start
  40.8 30.5 %copy.124 = bf16[72,8,16,512]{3,1,2,0:T(8,128)(2,1)} copy(bf16[72,8,16,512]{3,2,1,0:T(8,128)(2,1)} %bitcast.35) | data formatting | bytes 18874368
  71.3 5.6 fusion.24
  79.9 5.0 multiply_convert_fusion
  90.4 5.4 all_to_all.28
  95.8 9.4 %all-to-all-start = ((bf16[64,2,4096]{2,1,0:T(2,128)(2,1)}), bf16[64,2,4096]{2,1,0:T(2,128)(2,1)S(1)}, u32[]{:S(2)}, u32[]{:S(2)}) async-start(bf16[64,2,4096]{2,1,0:T(2,128)(2,1)} %reshape.146), calls=%async_computation | async-start | bytes 2097152 | tf_op jit(solution)/shard_map/all_to_all | solution.py:114
  108.7 5.0 copy.133
  113.8 5.8 reshape.150
  122.1 6.9 %all-to-all-start.2 = ((bf16[32,2,8192]{2,1,0:T(2,128)(2,1)}), bf16[32,2,8192]{2,1,0:T(2,128)(2,1)}, u32[]{:S(2)}, u32[]{:S(2)}) async-start(bf16[32,2,8192]{2,1,0:T(2,128)(2,1)} %reshape.150), calls=%async_computation.2 | async-start | bytes 2097152 | tf_op jit(solution)/shard_map/all_to_all | solution.py:43
  131.5 4.7 copy.97
  139.6 6.6 %copy.98 = f32[64,64,2,64]{3,0,2,1:T(8,128)} copy(f32[64,64,2,64]{3,1,0,2:T(8,128)} %bitcast.93) | data formatting | bytes 4194304 | tf_op jit(solution)/shard_map/convert_element_type | solution.py:128
  146.1 4.8 copy.116
  150.9 5.7 reshape.151
  163.6 5.4 concatenate.55
  172.0 6.3 pad_slice_fusion.6
  198.9 4.5 concatenate.52
  213.7 4.7 reshape.127
  234.6 13.3 %copy.117 = bf16[448,128,64]{0,2,1:T(8,128)(2,1)} copy(bf16[448,128,64]{1,2,0:T(8,128)(2,1)} %fusion.12) | data formatting | bytes 14680064 | tf_op jit(solution)/shard_map/concatenate | solution.py:86
  247.9 6.0 fusion
  261.6 4.8 reshape.152
  266.4 8.8 %all-to-all-start.3 = ((bf16[64,2,4096]{2,1,0:T(2,128)(2,1)}), bf16[64,2,4096]{2,1,0:T(2,128)(2,1)S(1)}, u32[]{:S(2)}, u32[]{:S(2)}) async-start(bf16[64,2,4096]{2,1,0:T(2,128)(2,1)} %reshape.152), calls=%async_computation.3 | async-start | bytes 2097152 | tf_op jit(solution)/shard_map/all_to_all | solution.py:136
  275.2 15.0 %dot_general.35 = bf16[9,64,8192]{2,1,0:T(8,128)(2,1)} reshape(bf16[576,2,8,512]{3,2,1,0:T(8,128)(2,1)} %slice_dynamic-update-slice_fusion.6) | data formatting | bytes 18874368 | tf_op jit(solution)/shard_map/dot_general | solution.py:98
  292.7 5.9 copy.121
  298.6 6.2 reshape.139
  304.9 7.7 %convolution_bitcast_fusion.2 = f32[7,64,64]{2,1,0:T(8,128)S(1)} fusion(bf16[7,64,8192]{2,1,0:T(8,128)(2,1)} %bitcast.95, f32[64,8192]{1,0:T(8,128)} %reshape.139, f32[64,8192]{1,0:T(8,128)} %convolution_bitcast_fusion), kind=kOutput, calls=%fused_computation.33 | convolution fusion | flops 474480640 | bytes 11649024 | tf_op jit(solution)/shard_map/dot_general | solution.py:98
  321.8 4.8 reshape.138
  326.5 4.8 reshape.137
  331.3 8.7 %convolution_bitcast_fusion.1 = f32[9,64,64]{2,1,0:T(8,128)S(1)} fusion(bf16[9,64,8192]{2,1,0:T(8,128)(2,1)} %dot_general.35, f32[64,8192]{1,0:T(8,128)} %reshape.138, f32[8192,64]{0,1:T(8,128)S(1)} %fusion.24), kind=kOutput, calls=%fused_computation.32 | convolution fusion | flops 608698368 | bytes 13778944 | tf_op jit(solution)/shard_map/dot_general | solution.py:98
  344.2 5.4 collective-permute-start.2
  350.9 252.6 %all-reduce.6.cloned.1.call-done = f32[65536]{0:T(1024)} async-done(((f32[65536]{0:T(1024)}), f32[65536]{0:T(1024)}) %all-reduce.6.cloned.1.call-update) | async-done | bytes 262160 | tf_op jit(solution)/shard_map/psum | solution.py:55
  618.3 18.5 %copy.126 = bf16[72,8,16,512]{3,1,2,0:T(8,128)(2,1)} copy(bf16[72,8,16,512]{3,2,1,0:T(8,128)(2,1)} %bitcast.101) | data formatting | bytes 18874368
  636.8 5.6 fusion.25
  (117 shorter events, 146.7 us)
Async XLA Ops:
  7.2 11.6 %copy-start.10 = (bf16[64,2,8,512]{3,2,1,0:T(8,128)(2,1)S(1)}, bf16[64,2,8,512]{3,2,1,0:T(8,128)(2,1)}, u32[]{:S(2)}) copy-start(bf16[64,2,8,512]{3,2,1,0:T(8,128)(2,1)} %param.5) | copy-start | bytes 3145732
  9.3 13.4 %collective-permute-start.1 = (bf16[64,2,1,512]{3,0,2,1:T(8,128)(2,1)S(1)}, bf16[64,2,1,512]{3,0,2,1:T(8,128)(2,1)S(1)}, u32[]{:S(2)}, u32[]{:S(2)}) collective-permute-start(bf16[64,2,1,512]{3,0,2,1:T(8,128)(2,1)S(1)} %copy.123), channel_id=1, source_target_pairs={{1,0},{2,1},{3,2},{5,4},{6,5},{7,6},{9,8},{10,9},{11,10},{13,12},{... | collective-permute-start | bytes 393224 | tf_op jit(solution)/shard_map/ppermute | solution.py:22
  11.3 11.6 %collective-permute-start = (bf16[64,2,1,512]{3,0,2,1:T(8,128)(2,1)}, bf16[64,2,1,512]{3,0,2,1:T(8,128)(2,1)}, u32[]{:S(2)}, u32[]{:S(2)}) collective-permute-start(bf16[64,2,1,512]{3,0,2,1:T(8,128)(2,1)} %copy.122), channel_id=1, source_target_pairs={{0,1},{1,2},{2,3},{4,5},{5,6},{6,7},{8,9},{9,10},{10,11},{12,13},{... | collective-permute-start | bytes 393224 | tf_op jit(solution)/shard_map/ppermute | solution.py:19
  20.4 3.6 copy-start.2
  95.8 26.3 %all-to-all-start = ((bf16[64,2,4096]{2,1,0:T(2,128)(2,1)}), bf16[64,2,4096]{2,1,0:T(2,128)(2,1)S(1)}, u32[]{:S(2)}, u32[]{:S(2)}) async-start(bf16[64,2,4096]{2,1,0:T(2,128)(2,1)} %reshape.146), calls=%async_computation | async-start | bytes 2097152 | tf_op jit(solution)/shard_map/all_to_all | solution.py:114
  113.8 15.2 %copy-start.13 = (bf16[7,64,64]{2,1,0:T(8,128)(2,1)S(1)}, bf16[7,64,64]{2,1,0:T(8,128)(2,1)}, u32[]{:S(2)}) copy-start(bf16[7,64,64]{2,1,0:T(8,128)(2,1)} %param.7) | copy-start | bytes 172036
  122.1 28.8 %all-to-all-start.2 = ((bf16[32,2,8192]{2,1,0:T(2,128)(2,1)}), bf16[32,2,8192]{2,1,0:T(2,128)(2,1)}, u32[]{:S(2)}, u32[]{:S(2)}) async-start(bf16[32,2,8192]{2,1,0:T(2,128)(2,1)} %reshape.150), calls=%async_computation.2 | async-start | bytes 2097152 | tf_op jit(solution)/shard_map/all_to_all | solution.py:43
  158.8 1.3 copy-start.3
  203.5 1.5 copy-start.9
  203.5 1.9 copy-start.8
  205.3 1.2 copy-start.7
  205.4 1.5 copy-start.6
  206.6 1.3 copy-start.5
  207.9 3.0 copy-start.1
  266.4 46.3 %all-to-all-start.3 = ((bf16[64,2,4096]{2,1,0:T(2,128)(2,1)}), bf16[64,2,4096]{2,1,0:T(2,128)(2,1)S(1)}, u32[]{:S(2)}, u32[]{:S(2)}) async-start(bf16[64,2,4096]{2,1,0:T(2,128)(2,1)} %reshape.152), calls=%async_computation.3 | async-start | bytes 2097152 | tf_op jit(solution)/shard_map/all_to_all | solution.py:136
  275.1 328.4 %all-reduce.6.cloned.1.call-start = ((), (), s32[]{:S(2)}) async-start(), calls=%async_computation.4 | async-start | bytes 524288 | tf_op jit(solution)/shard_map/psum | solution.py:55
  290.2 2.5 copy-start
  344.2 262.8 %collective-permute-start.2 = (bf16[64,2,1,512]{3,2,1,0:T(2,128)(2,1)S(1)}, bf16[64,2,1,512]{3,2,1,0:T(2,128)(2,1)S(1)}, u32[]{:S(2)}, u32[]{:S(2)}) collective-permute-start(bf16[64,2,1,512]{3,2,1,0:T(2,128)(2,1)S(1)} %get-tuple-element.9), channel_id=1, source_target_pairs={{0,1},{1,2},{2,3},{4,5},{5,6},{6,7},{8,9},{9,10},{10,11},{12,13},{... | collective-permute-start | bytes 393224 | tf_op jit(solution)/shard_map/ppermute | solution.py:19
  349.6 257.4 %collective-permute-start.3 = (bf16[64,2,1,512]{3,2,1,0:T(2,128)(2,1)S(1)}, bf16[64,2,1,512]{3,2,1,0:T(2,128)(2,1)S(1)}, u32[]{:S(2)}, u32[]{:S(2)}) collective-permute-start(bf16[64,2,1,512]{3,2,1,0:T(2,128)(2,1)S(1)} %get-tuple-element.10), channel_id=1, source_target_pairs={{1,0},{2,1},{3,2},{5,4},{6,5},{7,6},{9,8},{10,9},{11,10},{13,12},{... | collective-permute-start | bytes 393224 | tf_op jit(solution)/shard_map/ppermute | solution.py:22
  614.6 3.7 copy-start.4
  618.3 18.5 %copy-start.12 = (bf16[9,64,64]{2,1,0:T(8,128)(2,1)S(1)}, bf16[9,64,64]{2,1,0:T(8,128)(2,1)}, u32[]{:S(2)}) copy-start(bf16[9,64,64]{2,1,0:T(8,128)(2,1)} %param.6) | copy-start | bytes 221188
  642.4 1.2 copy-start.11
Sparse Core Ops, SparseCore 0:
  341.0 262.4 all-reduce.5
where the time goes:
time: 658 us; the launch traced here: 652 us
  local copies, waits for them, and re-layouts  273 us (41%)
  waiting for transfers between devices  255 us (39%)
  starting transfers between devices  39.5 us (6%)
  matrix products  36.3 us (6%)
  other arithmetic  28.4 us (4%)
  between operations  14.7 us (2%)
    psum x1, waiting for transfers between devices, packed_total(): so_far = lax.psum(ravelled, axis)  253 us
    unnamed x67, local copies, waits for them, and re-layouts  116 us
    concatenate x10, local copies, waits for them, and re-layouts, depth_stack(): return jnp.concatenate(pieces, axis=0)  45.5 us
    convert_element_type x5, local copies, waits for them, and re-layouts, on_device(): grad_pencil.astype(jnp.float32) * silu_slope(depth_output)  26.8 us
    dot_general x4, matrix products, stacked_mixing(): jnp.dot(weight, stacked.reshape(stacked.shape[0], -1), preferred_element_...  19.9 us
    dot_general x2, matrix products, stacked_kernel_grad(): jnp.dot(left.reshape(width, -1), stacked.reshape(stacked.shape[0], -1).T,...  16.4 us
    dot_general x1, local copies, waits for them, and re-layouts, stacked_kernel_grad(): jnp.dot(left.reshape(width, -1), stacked.reshape(stacked.shape[0], -1).T,...  15 us
    convert_element_type x3, local copies, waits for them, and re-layouts, on_device(): slab_grad.astype(jnp.float32) * silu_slope(pre_act)  14.1 us
  transfers between devices with their start and end apart: 8, of which 2 were waited for; matrix products, arithmetic and copies ran while one was open for 13% of the time, Pallas kernels for 0%

commit v1 on v0

v1 whole, which is shorter than its diff:
```python
import functools
import math

import jax
import jax.numpy as jnp
from jax import lax
from jax.experimental import pallas as pl
from jax.experimental.pallas import tpu as pltpu
from jax.sharding import Mesh
from jax.sharding import PartitionSpec as P

LANES = 128
SPREAD = ("wide_0", "wide_1", "wide_2")
WIDE = SPREAD + ("wide_3",)
FLAT = ("wide_0", "wide_1")
TALL = ("wide_2", "wide_3", "narrow")
FACTORS = (4, 4, 2, 2)


def group_size(axes):
    return math.prod(lax.axis_size(a) for a in axes)


def halo_rows(first, last, axis):
    count = lax.axis_size(axis)
    forward = [(i, i + 1) for i in range(count - 1)]
    backward = [(i + 1, i) for i in range(count - 1)]
    return lax.ppermute(last, axis, forward), lax.ppermute(first, axis, backward)


def sigmoid(v):
    return 1.0 / (1.0 + jnp.exp(-v))


def shifted(block, step):
    width = block.shape[1]
    lane = lax.broadcasted_iota(jnp.int32, block.shape, 1)
    edge = 0 if step == 1 else width - 1
    return jnp.where(lane == edge, 0.0, pltpu.roll(block, step % width, 1))


def fill_rows(rows_ref, vol_ref, low_ref, high_ref):
    slabs, rows, width, cols = vol_ref.shape
    for z in range(slabs):
        rows_ref[z, 0:width, :] = low_ref[z]
        rows_ref[z, (rows + 1) * width :, :] = high_ref[z]

        def copy(x, carry, z=z):
            rows_ref[z, pl.ds(pl.multiple_of((x + 1) * width, width), width), :] = vol_ref[z, x]
            return carry

        lax.fori_loop(0, rows, copy, 0)


def plane_forward_kernel(vol_ref, low_ref, high_ref, w_ref, act_ref, slope_ref, rows_ref):
    slabs, rows, width, cols = vol_ref.shape
    tiles = cols // LANES
    fill_rows(rows_ref, vol_ref, low_ref, high_ref)

    def step(n, carry):
        z, x = n // rows, n % rows
        window = rows_ref[z, pl.ds(pl.multiple_of(x * width, width), 3 * width), :]
        parts = jnp.dot(w_ref[...], window, preferred_element_type=jnp.float32)
        pre = (
            parts[width : 2 * width]
            + shifted(parts[:width], 1)
            + shifted(parts[2 * width :], -1)
        )
        gate = sigmoid(pre)
        slope_ref[z, x] = gate * (1.0 + pre * (1.0 - gate))
        act = (pre * gate).astype(jnp.bfloat16)
        for b in range(tiles):
            act_ref[x * tiles + b, z] = act[:, b * LANES : (b + 1) * LANES]
        return carry

    lax.fori_loop(0, slabs * rows, step, 0)


def depth_kernel(act_ref, grad_ref, wf_ref, wb_ref, out_ref, dw_ref, a_ref, d_ref, acc_ref):
    count, slabs, width, lanes = act_ref.shape
    rim = 3 * width
    cols = slabs * lanes
    zeros = jnp.zeros((rim, cols), jnp.bfloat16)
    for ref in (a_ref, d_ref):
        ref[0:rim, :] = zeros
        ref[rim + count * width :, :] = zeros
    acc_ref[...] = jnp.zeros_like(acc_ref)

    def fill(z, carry):
        for s in range(slabs):
            a_ref[
                pl.ds(pl.multiple_of(rim + z * width, width), width), s * lanes : (s + 1) * lanes
            ] = act_ref[z, s]
        return carry

    lax.fori_loop(0, count, fill, 0)

    def forward(n, carry):
        base = pl.multiple_of(n * 2 * width, 2 * width)
        window = a_ref[pl.ds(base, 8 * width), :]
        depth = jnp.dot(wf_ref[...], window, preferred_element_type=jnp.float32)
        gate = sigmoid(depth)
        slope = gate * (1.0 + depth * (1.0 - gate))
        for a in range(2):
            for s in range(slabs):
                part = slope[a * width : (a + 1) * width, s * lanes : (s + 1) * lanes]
                grad = grad_ref[2 * n + a, s].astype(jnp.float32) * part
                at = pl.multiple_of(rim + base + a * width, width)
                d_ref[pl.ds(at, width), s * lanes : (s + 1) * lanes] = grad.astype(jnp.bfloat16)
        return carry

    lax.fori_loop(0, count // 2, forward, 0)

    def backward(n, carry):
        base = pl.multiple_of(n * 2 * width, 2 * width)
        back = jnp.dot(
            wb_ref[...], d_ref[pl.ds(base, 8 * width), :], preferred_element_type=jnp.float32
        ).astype(jnp.bfloat16)
        for a in range(2):
            for s in range(slabs):
                out_ref[2 * n + a, s] = back[
                    a * width : (a + 1) * width, s * lanes : (s + 1) * lanes
                ]
        acc_ref[...] += lax.dot_general(
            d_ref[pl.ds(pl.multiple_of(rim + base, width), 2 * width), :],
            a_ref[pl.ds(base, 8 * width), :],
            (((1,), (1,)), ((), ())),
            preferred_element_type=jnp.float32,
        )
        return carry

    lax.fori_loop(0, count // 2, backward, 0)
    dw_ref[...] = acc_ref[0:width, :] + pltpu.roll(acc_ref[width:, :], 7 * width, 1)


def plane_grad_kernel(back_ref, slope_ref, rows_ref, dwz_ref, pre_ref, dw_ref, acc_ref):
    slabs, rows, width, cols = slope_ref.shape
    tiles = cols // LANES
    acc_ref[...] = jnp.zeros_like(acc_ref)

    def step(n, carry):
        z, x = n // rows, n % rows
        back = jnp.concatenate([back_ref[x * tiles + b, z] for b in range(tiles)], axis=1)
        grad = (back.astype(jnp.float32) * slope_ref[z, x]).astype(jnp.bfloat16)
        pre_ref[z, x] = grad
        wide = grad.astype(jnp.float32)
        stack = jnp.concatenate(
            [shifted(wide, -1).astype(jnp.bfloat16), grad, shifted(wide, 1).astype(jnp.bfloat16)],
            axis=0,
        )
        window = rows_ref[z, pl.ds(pl.multiple_of(x * width, width), 3 * width), :]
        acc_ref[...] += lax.dot_general(
            stack, window, (((1,), (1,)), ((), ())), preferred_element_type=jnp.float32
        )
        return carry

    lax.fori_loop(0, slabs * rows, step, 0)
    taps = [
        acc_ref[j * width : (j + 1) * width, i * width : (i + 1) * width]
        for i in range(3)
        for j in range(3)
    ] + [dwz_ref[:, k * width : (k + 1) * width] for k in range(7)]
    for p in range(8):
        dw_ref[p] = jnp.concatenate([taps[p], taps[p + 8]], axis=1)


def plane_backward_kernel(pre_ref, low_ref, high_ref, grad_ref, w_ref, out_ref, rows_ref):
    slabs, rows, width, cols = pre_ref.shape
    tiles = cols // LANES
    fill_rows(rows_ref, pre_ref, low_ref, high_ref)

    def step(n, carry):
        z, x = n // rows, n % rows
        window = rows_ref[z, pl.ds(pl.multiple_of(x * width, width), 3 * width), :]
        parts = jnp.dot(w_ref[...], window, preferred_element_type=jnp.float32)
        total = (
            parts[width : 2 * width]
            + shifted(parts[:width], -1)
            + shifted(parts[2 * width :], 1)
        )
        for b in range(tiles):
            lanes = slice(b * LANES, (b + 1) * LANES)
            grad = grad_ref[x * tiles + b, z].astype(jnp.float32)
            out_ref[z, x, :, lanes] = (total[:, lanes] + grad).astype(jnp.bfloat16)
        return carry

    lax.fori_loop(0, slabs * rows, step, 0)


def unpack_kernel(scale, total_ref, plane_ref, depth_ref):
    half = total_ref.shape[2] // 2
    for p in range(8):
        block = total_ref[p] * scale
        plane_ref[p] = block[:, :half]
        if p == 0:
            plane_ref[8] = block[:, half:]
        else:
            depth_ref[p - 1] = block[:, half:]


def call(kernel, name, outs, scratch=(), flops=0):
    vmem = pl.BlockSpec(memory_space=pltpu.VMEM)

    def run(*args):
        moved = sum(a.size * a.dtype.itemsize for a in (*args, *outs))
        return pl.pallas_call(
            kernel,
            out_shape=outs,
            in_specs=[vmem] * len(args),
            out_specs=[vmem] * len(outs),
            scratch_shapes=list(scratch),
            compiler_params=pltpu.CompilerParams(vmem_limit_bytes=40 << 20),
            cost_estimate=pl.CostEstimate(flops=flops, bytes_accessed=moved, transcendentals=0),
            name=name,
        )(*args)

    return run


def group_total(packed):
    first, second = group_size(FLAT), group_size(TALL)
    shape = packed.shape
    pieces = packed.reshape(first, -1, LANES)
    pieces = lax.all_to_all(pieces, FLAT, 0, 0, tiled=True)
    part = jnp.sum(pieces, axis=0)
    copies = jnp.broadcast_to(part[None], (second, *part.shape))
    part = jnp.sum(lax.all_to_all(copies, TALL, 0, 0, tiled=True), axis=0)
    copies = jnp.broadcast_to(part[None], (first, *part.shape))
    return lax.all_to_all(copies, FLAT, 0, 0, tiled=True).reshape(shape)


def on_device(volume, out_grad, plane_kernel, z_axis_kernel):
    width, slabs, rows, cols = volume.shape
    tiles = cols // LANES
    peers = group_size(SPREAD)
    shape = jax.ShapeDtypeStruct
    bf16, f32 = jnp.bfloat16, jnp.float32
    gradient_scale = 1.0 / math.sqrt(
        slabs * group_size(WIDE) * rows * lax.axis_size("narrow") * cols
    )
    blocks = (rows * tiles, slabs, width, LANES)

    grad_blocks = out_grad.reshape(width, slabs, rows, tiles, LANES)
    grad_blocks = grad_blocks.transpose(2, 3, 1, 0, 4).reshape(blocks)
    grad_pencil = lax.all_to_all(grad_blocks, SPREAD, 0, 0, tiled=True)

    taps = plane_kernel.reshape(3, 3, width, width)
    plane_forward = taps.transpose(1, 2, 0, 3).reshape(3 * width, 3 * width)
    plane_backward = taps[::-1].transpose(1, 3, 0, 2).reshape(3 * width, 3 * width)
    none = jnp.zeros((1, width, width), bf16)

    def banded(tap_list):
        upper = jnp.concatenate([tap_list, none]).transpose(1, 0, 2).reshape(width, -1)
        lower = jnp.concatenate([none, tap_list]).transpose(1, 0, 2).reshape(width, -1)
        return jnp.concatenate([upper, lower])

    depth_forward = banded(z_axis_kernel)
    depth_backward = banded(z_axis_kernel[::-1].transpose(0, 2, 1))

    slab = volume.transpose(1, 2, 0, 3)
    low, high = halo_rows(slab[:, 0], slab[:, rows - 1], "narrow")
    plane_flops = 2 * 9 * width * width * slabs * rows * cols
    depth_flops = plane_flops * 7 // 9
    act, slope, rimmed = call(
        plane_forward_kernel,
        "plane_forward",
        (
            shape(blocks, bf16),
            shape((slabs, rows, width, cols), f32),
            shape((slabs, (rows + 2) * width, cols), bf16),
        ),
        flops=plane_flops,
    )(slab, low, high, plane_forward)

    act_pencil = lax.all_to_all(act, SPREAD, 0, 0, tiled=True)
    span = (peers + 6) * width
    back_pencil, depth_term = call(
        depth_kernel,
        "depth",
        (shape(act_pencil.shape, bf16), shape((width, 8 * width), f32)),
        (
            pltpu.VMEM((span, slabs * LANES), bf16),
            pltpu.VMEM((span, slabs * LANES), bf16),
            pltpu.VMEM((2 * width, 8 * width), f32),
        ),
        flops=3 * depth_flops,
    )(act_pencil, grad_pencil, depth_forward, depth_backward)
    back = lax.all_to_all(back_pencil, SPREAD, 0, 0, tiled=True)

    pre_grad, packed = call(
        plane_grad_kernel,
        "plane_grad",
        (shape((slabs, rows, width, cols), bf16), shape((8, width, 2 * width), f32)),
        (pltpu.VMEM((3 * width, 3 * width), f32),),
        flops=plane_flops,
    )(back, slope, rimmed, depth_term)
    low, high = halo_rows(pre_grad[:, 0], pre_grad[:, rows - 1], "narrow")
    total = group_total(packed)
    (volume_grad,) = call(
        plane_backward_kernel,
        "plane_backward",
        (shape((slabs, rows, width, cols), bf16),),
        (pltpu.VMEM((slabs, (rows + 2) * width, cols), bf16),),
        flops=plane_flops,
    )(pre_grad, low, high, grad_blocks, plane_backward)
    plane_total, depth_total = call(
        functools.partial(unpack_kernel, gradient_scale),
        "unpack",
        (shape((9, width, width), f32), shape((7, width, width), f32)),
    )(total)
    return volume_grad.transpose(2, 0, 1, 3), plane_total, depth_total


def solution(mesh):
    names = WIDE + ("narrow",)
    finer = Mesh(mesh.devices.reshape(*FACTORS, mesh.shape["narrow"]), names)
    return jax.shard_map(
        on_device,
        mesh=finer,
        in_specs=(P(None, WIDE, "narrow", None), P(None, WIDE, "narrow", None), P(), P()),
        out_specs=(P(None, WIDE, "narrow", None), P(), P()),
        check_vma=False,
    )
```

time: 658 us -> 157 us (0.24)
  local copies, waits for them, and re-layouts: 273 us -> 16.1 us
  waiting for transfers between devices: 255 us -> 23.3 us
  blocking collectives: 5.37 us -> 46.2 us
  matrix products: 36.3 us -> 0 us
  other arithmetic: 28.4 us -> 0.94 us
  Pallas kernels: 0 us -> 26.5 us
  between operations: 14.7 us -> 0.88 us
    psum x1 -> x0, waiting for transfers between devices: 253 us -> none  [packed_total(): so_far = lax.psum(ravelled, axis)]
    unnamed x67 -> x24, local copies, waits for them, and re-layouts: 116 us -> 7.3 us
    convert_element_type x10 -> x0, local copies, waits for them, and re-layouts: 48.5 us -> none  [the longest x5 26.8 us: on_device(): grad_pencil.astype(jnp.float32) * silu_slope(depth_output)]
    concatenate x12 -> x1, local copies, waits for them, and re-layouts: 47.4 us -> 0.04 us  [banded(): jnp.concatenate([tap_list, none]).transpose(1, 0, 2).reshape(width, -1)]
    all_to_all x1 -> x3, blocking collectives: 5.37 us -> 46.2 us  [the longest x1 18.7 us: on_device(): back = lax.all_to_all(back_pencil, SPREAD, 0, 0, tiled=True)]
    dot_general x6 -> x0, matrix products: 36.3 us -> none  [the longest x4 19.9 us: stacked_mixing(): jnp.dot(weight, stacked.reshape(stacked.shape[0], -1), preferred_element_...]
    pallas_call x0 -> x5, Pallas kernels: none -> 26.5 us  [run(): pl.pallas_call(kernel, out_shape=outs, in_specs=[vmem] * len(args), out_s...]
    dot_general x1 -> x0, local copies, waits for them, and re-layouts: 15 us -> none  [stacked_kernel_grad(): jnp.dot(left.reshape(width, -1), stacked.reshape(stacked.shape[0], -1).T,...]
  transfers between devices with their start and end apart: 8 -> 7, of which waited for: 2 -> 4; matrix products, arithmetic and copies ran while one was open for 13% -> 5% of each run, Pallas kernels for 0% -> 7%
where the time goes in v1:
time: 157 us; the launch traced here: 155 us
  blocking collectives  46.2 us (29%)
  starting transfers between devices  41.1 us (26%)
  Pallas kernels  26.5 us (17%)
  waiting for transfers between devices  23.3 us (15%)
  local copies, waits for them, and re-layouts  16.1 us (10%)
    pallas_call x5, Pallas kernels, run(): pl.pallas_call(kernel, out_shape=outs, in_specs=[vmem] * len(args), out_s...  26.5 us
    all_to_all x1, blocking collectives, on_device(): back = lax.all_to_all(back_pencil, SPREAD, 0, 0, tiled=True)  18.7 us
    all_to_all x1, blocking collectives, group_total(): part = jnp.sum(lax.all_to_all(copies, TALL, 0, 0, tiled=True), axis=0)  14.9 us
    all_to_all x1, starting transfers between devices, on_device(): act_pencil = lax.all_to_all(act, SPREAD, 0, 0, tiled=True)  14.5 us
    all_to_all x1, blocking collectives, group_total(): pieces = lax.all_to_all(pieces, FLAT, 0, 0, tiled=True)  12.6 us
    all_to_all x1, waiting for transfers between devices, on_device(): act_pencil = lax.all_to_all(act, SPREAD, 0, 0, tiled=True)  10 us
    ppermute x2, starting transfers between devices, halo_rows(): lax.ppermute(last, axis, forward)  9.7 us
    all_to_all x1, starting transfers between devices, on_device(): grad_pencil = lax.all_to_all(grad_blocks, SPREAD, 0, 0, tiled=True)  8.98 us
  transfers between devices with their start and end apart: 7, of which 4 were waited for; matrix products, arithmetic and copies ran while one was open for 5% of the time, Pallas kernels for 7%

profile of v1, /device:TPU:2, one launch (start us, length us, event | category | flops | bytes accessed | tf_op | source)
XLA Modules:
  0.0 155.0 jit_solution(16421662608138467880)
XLA Ops:
  0.6 3.0 %copy.34 = bf16[64,2,8,4,128]{4,0,1,3,2:T(8,128)(2,1)} copy(bf16[64,2,8,4,128]{4,2,3,1,0:T(8,128)(2,1)} %bitcast.41) | data formatting | bytes 2097152 | tf_op jit(solution)/shard_map/reshape | solution.py:243
  3.6 9.0 %all-to-all-start.1 = ((bf16[32,2,64,128]{3,2,1,0:T(8,128)(2,1)}), bf16[32,2,64,128]{3,2,1,0:T(8,128)(2,1)S(1)}, u32[]{:S(2)}, u32[]{:S(2)}) async-start(bf16[32,2,64,128]{3,2,1,0:T(8,128)(2,1)} %bitcast.8.grad_ref), calls=%async_computation.1 | async-start | bytes 2097152 | tf_op jit(solution)/shard_map/all_to_all | solution.py:245
  13.2 5.2 %collective-permute-start = (bf16[2,64,512]{2,1,0:T(8,128)(2,1)S(1)}, bf16[2,64,512]{2,1,0:T(8,128)(2,1)S(1)}, u32[]{:S(2)}, u32[]{:S(2)}) collective-permute-start(bf16[2,64,512]{2,1,0:T(8,128)(2,1)S(1)} %get-tuple-element.33), channel_id=1, source_target_pairs={{0,1},{1,2},{2,3},{4,5},{5,6},{6,7},{8,9},{9,10},{10,11},{12,13},{... | collective-permute-start | bytes 393224 | tf_op jit(solution)/shard_map/ppermute | solution.py:28
  18.4 1.3 collective-permute-start.1
  20.6 5.8 %collective-permute-done.low_ref = bf16[2,64,512]{2,1,0:T(8,128)(2,1)S(1)} collective-permute-done((bf16[2,64,512]{2,1,0:T(8,128)(2,1)S(1)}, bf16[2,64,512]{2,1,0:T(8,128)(2,1)S(1)}, u32[]{:S(2)}, u32[]{:S(2)}) %collective-permute-start) | collective-permute-done | bytes 131104 | tf_op jit(solution)/shard_map/ppermute | solution.py:28
  26.9 5.4 %plane_forward.1 = (bf16[32,2,64,128]{3,2,1,0:T(8,128)(2,1)S(1)}, f32[2,8,64,512]{3,2,1,0:T(8,128)S(1)}, bf16[2,640,512]{2,1,0:T(8,128)(2,1)S(1)}) custom-call(bf16[2,8,64,512]{3,2,1,0:T(8,128)(2,1)S(1)} %copy.33.vol_ref, bf16[2,64,512]{2,1,0:T(8,128)(2,1)S(1)} %collective-permute-done.low_ref, bf16[2,64,512]{2,1,0:T(8,128)(2,1)S(1)} %collective-permute-done.1.high_ref, ...), custom_call_target="tpu_custom_call" | custom-call | flops 603979776 | bytes 5840896 | tf_op jit(solution)/shard_map/plane_forward/pallas_call | solution.py:206
  32.3 1.1 copy-done
  33.4 1.0 copy-done.2
  34.3 14.5 %all-to-all-start = ((bf16[32,2,64,128]{3,2,1,0:T(8,128)(2,1)}), bf16[32,2,64,128]{3,2,1,0:T(8,128)(2,1)}, u32[]{:S(2)}, u32[]{:S(2)}) async-start(bf16[32,2,64,128]{3,2,1,0:T(8,128)(2,1)} %copy-done.2), calls=%async_computation | async-start | bytes 2097152 | tf_op jit(solution)/shard_map/all_to_all | solution.py:275
  48.9 1.0 pad_bitcast_fusion.1
  50.0 0.8 reshape.45
  50.9 0.8 reshape.46
  51.9 0.9 pad_maximum_fusion
  52.8 10.0 %all-to-all-done.act_ref = bf16[32,2,64,128]{3,2,1,0:T(8,128)(2,1)} async-done(((bf16[32,2,64,128]{3,2,1,0:T(8,128)(2,1)}), bf16[32,2,64,128]{3,2,1,0:T(8,128)(2,1)}, u32[]{:S(2)}, u32[]{:S(2)}) %all-to-all-start) | async-done | bytes 1048608 | tf_op jit(solution)/shard_map/all_to_all | solution.py:275
  62.8 9.8 %depth.1 = (bf16[32,2,64,128]{3,2,1,0:T(8,128)(2,1)S(1)}, f32[64,512]{1,0:T(8,128)S(1)}) custom-call(bf16[32,2,64,128]{3,2,1,0:T(8,128)(2,1)} %all-to-all-done.act_ref, bf16[32,2,64,128]{3,2,1,0:T(8,128)(2,1)S(1)} %all-to-all-done.1.grad_ref, bf16[128,512]{1,0:T(8,128)(2,1)S(1)} %get-tuple-element.38.wf_ref, bf16[128,512]{1,0:T(8,128)(2,1)S(1)} %get-tuple-element.39.wb_ref), custom_call_target="tpu_custom_call" | custom-call | flops 1409286144 | bytes 3538944 | tf_op jit(solution)/shard_map/depth/pallas_call | solution.py:206
  72.6 18.7 %all_to_all.30.back_ref = bf16[32,2,64,128]{3,2,1,0:T(8,128)(2,1)S(1)} all-to-all(bf16[32,2,64,128]{3,2,1,0:T(8,128)(2,1)S(1)} %get-tuple-element.13), channel_id=1, replica_groups=mesh['wide_0'=4,'wide_1'=4,'wide_2'=2,'wide_3'=2,'narrow'=4] {'wide_0','..., dimensions={0} | all-to-all | bytes 2097152 | tf_op jit(solution)/shard_map/all_to_all | solution.py:288
  91.3 4.4 %plane_grad.1 = (bf16[2,8,64,512]{3,2,1,0:T(8,128)(2,1)S(1)}, f32[8,64,128]{2,1,0:T(8,128)S(1)}) custom-call(bf16[32,2,64,128]{3,2,1,0:T(8,128)(2,1)S(1)} %all_to_all.30.back_ref, f32[2,8,64,512]{3,2,1,0:T(8,128)S(1)} %get-tuple-element.14.slope_ref, bf16[2,640,512]{2,1,0:T(8,128)(2,1)S(1)} %copy-done.1, f32[64,512]{1,0:T(8,128)S(1)} %get-tuple-element.16.dwz_ref), custom_call_target="tpu_custom_call" | custom-call | flops 603979776 | bytes 5898240 | tf_op jit(solution)/shard_map/plane_grad/pallas_call | solution.py:206
  95.7 12.6 %all_to_all.31 = f32[16,32,128]{2,1,0:T(8,128)S(1)} all-to-all(f32[16,32,128]{2,1,0:T(8,128)S(1)} %bitcast.38), channel_id=1, replica_groups=mesh['wide_0'=4,'wide_1'=4,'wide_2'=2,'wide_3'=2,'narrow'=4] {'wide_0','..., dimensions={0} | all-to-all | bytes 524288 | tf_op jit(solution)/shard_map/all_to_all | solution.py:224
  108.4 14.9 %all_to_all.32 = f32[16,32,128]{2,1,0:T(8,128)S(1)} all-to-all(f32[16,32,128]{2,1,0:T(8,128)S(1)} %broadcast_in_dim.4), channel_id=1, replica_groups=mesh['wide_0'=4,'wide_1'=4,'wide_2'=2,'wide_3'=2,'narrow'=4] {'wide_2','..., dimensions={0} | all-to-all | bytes 524288 | tf_op jit(solution)/shard_map/all_to_all | solution.py:227
  123.3 0.7 broadcast_in_dim.5
  124.0 5.3 %all-to-all-start.5 = ((f32[16,32,128]{2,1,0:T(8,128)}), f32[16,32,128]{2,1,0:T(8,128)S(1)}, u32[]{:S(2)}, u32[]{:S(2)}) async-start(f32[16,32,128]{2,1,0:T(8,128)} %broadcast_in_dim.5), calls=%async_computation.5 | async-start | bytes 524288 | tf_op jit(solution)/shard_map/all_to_all | solution.py:229
  129.4 4.5 %collective-permute-start.2 = (bf16[2,64,512]{2,1,0:T(8,128)(2,1)S(1)}, bf16[2,64,512]{2,1,0:T(8,128)(2,1)S(1)}, u32[]{:S(2)}, u32[]{:S(2)}) collective-permute-start(bf16[2,64,512]{2,1,0:T(8,128)(2,1)S(1)} %get-tuple-element.31), channel_id=1, source_target_pairs={{0,1},{1,2},{2,3},{4,5},{5,6},{6,7},{8,9},{9,10},{10,11},{12,13},{... | collective-permute-start | bytes 393224 | tf_op jit(solution)/shard_map/ppermute | solution.py:28
  133.9 1.3 collective-permute-start.3
  135.4 0.8 rev.7
  136.4 0.7 copy-done.3
  137.0 7.0 %collective-permute-done.3.high_ref = bf16[2,64,512]{2,1,0:T(8,128)(2,1)S(1)} collective-permute-done((bf16[2,64,512]{2,1,0:T(8,128)(2,1)S(1)}, bf16[2,64,512]{2,1,0:T(8,128)(2,1)S(1)}, u32[]{:S(2)}, u32[]{:S(2)}) %collective-permute-start.3) | collective-permute-done | bytes 131104 | tf_op jit(solution)/shard_map/ppermute | solution.py:28
  144.0 0.7 copy-done.5
  144.7 0.9 copy-done.4
  145.6 0.9 copy-done.6
  146.5 6.1 %plane_backward.1 = bf16[2,8,64,512]{3,2,1,0:T(8,128)(2,1)S(1)} custom-call(bf16[2,8,64,512]{3,2,1,0:T(8,128)(2,1)S(1)} %get-tuple-element.17.pre_ref, bf16[2,64,512]{2,1,0:T(8,128)(2,1)S(1)} %copy-done.4, bf16[2,64,512]{2,1,0:T(8,128)(2,1)S(1)} %copy-done.6, bf16[32,2,64,128]{3,2,1,0:T(8,128)(2,1)} %bitcast.8.grad_ref, bf16[192,192]{1,0:T(8,128)(2,1)S(1)} %reshape.49.w_ref), custom_call_target="tpu_custom_call" | custom-call | flops 603979776 | bytes 3481600 | tf_op jit(solution)/shard_map/plane_backward/pallas_call | solution.py:206
  152.6 1.5 copy.42
  154.2 0.9 unpack.1
  (37 shorter events, 2.9 us)
Async XLA Ops:
  0.6 12.0 %copy-start.7 = (bf16[64,2,8,512]{3,2,1,0:T(8,128)(2,1)S(1)}, bf16[64,2,8,512]{3,2,1,0:T(8,128)(2,1)}, u32[]{:S(2)}) copy-start(bf16[64,2,8,512]{3,2,1,0:T(8,128)(2,1)} %param.4) | copy-start | bytes 3145732
  3.6 30.7 %all-to-all-start.1 = ((bf16[32,2,64,128]{3,2,1,0:T(8,128)(2,1)}), bf16[32,2,64,128]{3,2,1,0:T(8,128)(2,1)S(1)}, u32[]{:S(2)}, u32[]{:S(2)}) async-start(bf16[32,2,64,128]{3,2,1,0:T(8,128)(2,1)} %bitcast.8.grad_ref), calls=%async_computation.1 | async-start | bytes 2097152 | tf_op jit(solution)/shard_map/all_to_all | solution.py:245
  12.6 7.1 %copy-start.8 = (bf16[9,64,64]{2,1,0:T(8,128)(2,1)S(1)}, bf16[9,64,64]{2,1,0:T(8,128)(2,1)}, u32[]{:S(2)}) copy-start(bf16[9,64,64]{2,1,0:T(8,128)(2,1)} %param.6) | copy-start | bytes 221188
  13.2 13.2 %collective-permute-start = (bf16[2,64,512]{2,1,0:T(8,128)(2,1)S(1)}, bf16[2,64,512]{2,1,0:T(8,128)(2,1)S(1)}, u32[]{:S(2)}, u32[]{:S(2)}) collective-permute-start(bf16[2,64,512]{2,1,0:T(8,128)(2,1)S(1)} %get-tuple-element.33), channel_id=1, source_target_pairs={{0,1},{1,2},{2,3},{4,5},{5,6},{6,7},{8,9},{9,10},{10,11},{12,13},{... | collective-permute-start | bytes 393224 | tf_op jit(solution)/shard_map/ppermute | solution.py:28
  18.4 8.5 %collective-permute-start.1 = (bf16[2,64,512]{2,1,0:T(8,128)(2,1)S(1)}, bf16[2,64,512]{2,1,0:T(8,128)(2,1)S(1)}, u32[]{:S(2)}, u32[]{:S(2)}) collective-permute-start(bf16[2,64,512]{2,1,0:T(8,128)(2,1)S(1)} %get-tuple-element.32), channel_id=1, source_target_pairs={{1,0},{2,1},{3,2},{5,4},{6,5},{7,6},{9,8},{10,9},{11,10},{13,12},{... | collective-permute-start | bytes 393224 | tf_op jit(solution)/shard_map/ppermute | solution.py:28
  32.3 1.1 copy-start
  33.4 1.0 copy-start.2
  34.3 17.3 %copy-start.10 = (bf16[7,64,64]{2,1,0:T(8,128)(2,1)S(1)}, bf16[7,64,64]{2,1,0:T(8,128)(2,1)}, u32[]{:S(2)}) copy-start(bf16[7,64,64]{2,1,0:T(8,128)(2,1)} %param.7) | copy-start | bytes 172036
  34.3 28.5 %all-to-all-start = ((bf16[32,2,64,128]{3,2,1,0:T(8,128)(2,1)}), bf16[32,2,64,128]{3,2,1,0:T(8,128)(2,1)}, u32[]{:S(2)}, u32[]{:S(2)}) async-start(bf16[32,2,64,128]{3,2,1,0:T(8,128)(2,1)} %copy-done.2), calls=%async_computation | async-start | bytes 2097152 | tf_op jit(solution)/shard_map/all_to_all | solution.py:275
  72.6 18.7 %copy-start.1 = (bf16[2,640,512]{2,1,0:T(8,128)(2,1)S(1)}, bf16[2,640,512]{2,1,0:T(8,128)(2,1)}, u32[]{:S(2)}) copy-start(bf16[2,640,512]{2,1,0:T(8,128)(2,1)} %copy-done) | copy-start | bytes 3932164
  95.7 39.5 %copy-start.9 = (bf16[9,64,64]{2,1,0:T(8,128)(2,1)S(1)}, bf16[9,64,64]{2,1,0:T(8,128)(2,1)}, u32[]{:S(2)}) copy-start(bf16[9,64,64]{2,1,0:T(8,128)(2,1)} %param.6) | copy-start | bytes 221188
  124.0 30.2 %all-to-all-start.5 = ((f32[16,32,128]{2,1,0:T(8,128)}), f32[16,32,128]{2,1,0:T(8,128)S(1)}, u32[]{:S(2)}, u32[]{:S(2)}) async-start(f32[16,32,128]{2,1,0:T(8,128)} %broadcast_in_dim.5), calls=%async_computation.5 | async-start | bytes 524288 | tf_op jit(solution)/shard_map/all_to_all | solution.py:229
  129.4 7.0 %collective-permute-start.2 = (bf16[2,64,512]{2,1,0:T(8,128)(2,1)S(1)}, bf16[2,64,512]{2,1,0:T(8,128)(2,1)S(1)}, u32[]{:S(2)}, u32[]{:S(2)}) collective-permute-start(bf16[2,64,512]{2,1,0:T(8,128)(2,1)S(1)} %get-tuple-element.31), channel_id=1, source_target_pairs={{0,1},{1,2},{2,3},{4,5},{5,6},{6,7},{8,9},{9,10},{10,11},{12,13},{... | collective-permute-start | bytes 393224 | tf_op jit(solution)/shard_map/ppermute | solution.py:28
  133.9 10.1 %collective-permute-start.3 = (bf16[2,64,512]{2,1,0:T(8,128)(2,1)S(1)}, bf16[2,64,512]{2,1,0:T(8,128)(2,1)S(1)}, u32[]{:S(2)}, u32[]{:S(2)}) collective-permute-start(bf16[2,64,512]{2,1,0:T(8,128)(2,1)S(1)} %get-tuple-element.30), channel_id=1, source_target_pairs={{1,0},{2,1},{3,2},{5,4},{6,5},{7,6},{9,8},{10,9},{11,10},{13,12},{... | collective-permute-start | bytes 393224 | tf_op jit(solution)/shard_map/ppermute | solution.py:28
  136.4 0.7 copy-start.3
  144.0 0.7 copy-start.5
  144.7 0.9 copy-start.4
  145.6 0.9 copy-start.6

commit v2 on v1

--- a/solution.py
+++ b/solution.py
@@ -10,6 +10,7 @@
 from jax.sharding import PartitionSpec as P
 
 LANES = 128
+UNROLL = 8
 SPREAD = ("wide_0", "wide_1", "wide_2")
 WIDE = SPREAD + ("wide_3",)
 FLAT = ("wide_0", "wide_1")
@@ -40,7 +41,7 @@
 
 
 def fill_rows(rows_ref, vol_ref, low_ref, high_ref):
-    slabs, rows, width, cols = vol_ref.shape
+    slabs, rows, width, _ = vol_ref.shape
     for z in range(slabs):
         rows_ref[z, 0:width, :] = low_ref[z]
         rows_ref[z, (rows + 1) * width :, :] = high_ref[z]
@@ -49,10 +50,12 @@
             rows_ref[z, pl.ds(pl.multiple_of((x + 1) * width, width), width), :] = vol_ref[z, x]
             return carry
 
-        lax.fori_loop(0, rows, copy, 0)
-
-
-def plane_forward_kernel(vol_ref, low_ref, high_ref, w_ref, act_ref, slope_ref, rows_ref):
+        lax.fori_loop(0, rows, copy, 0, unroll=True)
+
+
+def plane_forward_kernel(
+    vol_ref, low_ref, high_ref, w_ref, grad_ref, both_ref, slope_ref, rows_ref
+):
     slabs, rows, width, cols = vol_ref.shape
     tiles = cols // LANES
     fill_rows(rows_ref, vol_ref, low_ref, high_ref)
@@ -70,14 +73,15 @@
         slope_ref[z, x] = gate * (1.0 + pre * (1.0 - gate))
         act = (pre * gate).astype(jnp.bfloat16)
         for b in range(tiles):
-            act_ref[x * tiles + b, z] = act[:, b * LANES : (b + 1) * LANES]
-        return carry
-
-    lax.fori_loop(0, slabs * rows, step, 0)
-
-
-def depth_kernel(act_ref, grad_ref, wf_ref, wb_ref, out_ref, dw_ref, a_ref, d_ref, acc_ref):
-    count, slabs, width, lanes = act_ref.shape
+            both_ref[x * tiles + b, z] = act[:, b * LANES : (b + 1) * LANES]
+            both_ref[x * tiles + b, slabs + z] = grad_ref[x * tiles + b, z]
+        return carry
+
+    lax.fori_loop(0, slabs * rows, step, 0, unroll=UNROLL)
+
+
+def depth_kernel(both_ref, wf_ref, wb_ref, out_ref, dw_ref, a_ref, d_ref, acc_ref):
+    count, slabs, width, lanes = out_ref.shape
     rim = 3 * width
     cols = slabs * lanes
     zeros = jnp.zeros((rim, cols), jnp.bfloat16)
@@ -90,10 +94,10 @@
         for s in range(slabs):
             a_ref[
                 pl.ds(pl.multiple_of(rim + z * width, width), width), s * lanes : (s + 1) * lanes
-            ] = act_ref[z, s]
-        return carry
-
-    lax.fori_loop(0, count, fill, 0)
+            ] = both_ref[z, s]
+        return carry
+
+    lax.fori_loop(0, count, fill, 0, unroll=4)
 
     def forward(n, carry):
         base = pl.multiple_of(n * 2 * width, 2 * width)
@@ -104,12 +108,12 @@
         for a in range(2):
             for s in range(slabs):
                 part = slope[a * width : (a + 1) * width, s * lanes : (s + 1) * lanes]
-                grad = grad_ref[2 * n + a, s].astype(jnp.float32) * part
+                grad = both_ref[2 * n + a, slabs + s].astype(jnp.float32) * part
                 at = pl.multiple_of(rim + base + a * width, width)
                 d_ref[pl.ds(at, width), s * lanes : (s + 1) * lanes] = grad.astype(jnp.bfloat16)
         return carry
 
-    lax.fori_loop(0, count // 2, forward, 0)
+    lax.fori_loop(0, count // 2, forward, 0, unroll=UNROLL)
 
     def backward(n, carry):
         base = pl.multiple_of(n * 2 * width, 2 * width)
@@ -129,7 +133,7 @@
         )
         return carry
 
-    lax.fori_loop(0, count // 2, backward, 0)
+    lax.fori_loop(0, count // 2, backward, 0, unroll=UNROLL)
     dw_ref[...] = acc_ref[0:width, :] + pltpu.roll(acc_ref[width:, :], 7 * width, 1)
 
 
@@ -154,7 +158,7 @@
         )
         return carry
 
-    lax.fori_loop(0, slabs * rows, step, 0)
+    lax.fori_loop(0, slabs * rows, step, 0, unroll=UNROLL)
     taps = [
         acc_ref[j * width : (j + 1) * width, i * width : (i + 1) * width]
         for i in range(3)
@@ -184,7 +188,7 @@
             out_ref[z, x, :, lanes] = (total[:, lanes] + grad).astype(jnp.bfloat16)
         return carry
 
-    lax.fori_loop(0, slabs * rows, step, 0)
+    lax.fori_loop(0, slabs * rows, step, 0, unroll=UNROLL)
 
 
 def unpack_kernel(scale, total_ref, plane_ref, depth_ref):
@@ -198,7 +202,7 @@
             depth_ref[p - 1] = block[:, half:]
 
 
-def call(kernel, name, outs, scratch=(), flops=0):
+def call(kernel, outs, scratch=(), flops=0):
     vmem = pl.BlockSpec(memory_space=pltpu.VMEM)
 
     def run(*args):
@@ -209,24 +213,21 @@
             in_specs=[vmem] * len(args),
             out_specs=[vmem] * len(outs),
             scratch_shapes=list(scratch),
-            compiler_params=pltpu.CompilerParams(vmem_limit_bytes=40 << 20),
+            compiler_params=pltpu.CompilerParams(vmem_limit_bytes=16 << 20),
             cost_estimate=pl.CostEstimate(flops=flops, bytes_accessed=moved, transcendentals=0),
-            name=name,
         )(*args)
 
     return run
 
 
-def group_total(packed):
-    first, second = group_size(FLAT), group_size(TALL)
-    shape = packed.shape
-    pieces = packed.reshape(first, -1, LANES)
-    pieces = lax.all_to_all(pieces, FLAT, 0, 0, tiled=True)
+def spread_pieces(packed):
+    pieces = packed.reshape(group_size(FLAT), -1, LANES)
+    return lax.all_to_all(pieces, FLAT, 0, 0, tiled=True)
+
+
+def copies_of(pieces, count):
     part = jnp.sum(pieces, axis=0)
-    copies = jnp.broadcast_to(part[None], (second, *part.shape))
-    part = jnp.sum(lax.all_to_all(copies, TALL, 0, 0, tiled=True), axis=0)
-    copies = jnp.broadcast_to(part[None], (first, *part.shape))
-    return lax.all_to_all(copies, FLAT, 0, 0, tiled=True).reshape(shape)
+    return jnp.broadcast_to(part[None], (count, *part.shape))
 
 
 def on_device(volume, out_grad, plane_kernel, z_axis_kernel):
@@ -240,9 +241,13 @@
     )
     blocks = (rows * tiles, slabs, width, LANES)
 
+    slab = volume.transpose(1, 2, 0, 3)
+    first, last = slab[:, 0], slab[:, rows - 1]
+    low, high = halo_rows(first, last, "narrow")
+
+
     grad_blocks = out_grad.reshape(width, slabs, rows, tiles, LANES)
     grad_blocks = grad_blocks.transpose(2, 3, 1, 0, 4).reshape(blocks)
-    grad_pencil = lax.all_to_all(grad_blocks, SPREAD, 0, 0, tiled=True)
 
     taps = plane_kernel.reshape(3, 3, width, width)
     plane_forward = taps.transpose(1, 2, 0, 3).reshape(3 * width, 3 * width)
@@ -257,58 +262,59 @@
     depth_forward = banded(z_axis_kernel)
     depth_backward = banded(z_axis_kernel[::-1].transpose(0, 2, 1))
 
-    slab = volume.transpose(1, 2, 0, 3)
-    low, high = halo_rows(slab[:, 0], slab[:, rows - 1], "narrow")
     plane_flops = 2 * 9 * width * width * slabs * rows * cols
     depth_flops = plane_flops * 7 // 9
-    act, slope, rimmed = call(
+    low, high, plane_forward, depth_forward, depth_backward = lax.optimization_barrier(
+        (low, high, plane_forward, depth_forward, depth_backward)
+    )
+    both, slope, rimmed = call(
         plane_forward_kernel,
-        "plane_forward",
         (
-            shape(blocks, bf16),
+            shape((blocks[0], 2 * slabs, width, LANES), bf16),
             shape((slabs, rows, width, cols), f32),
             shape((slabs, (rows + 2) * width, cols), bf16),
         ),
         flops=plane_flops,
-    )(slab, low, high, plane_forward)
-
-    act_pencil = lax.all_to_all(act, SPREAD, 0, 0, tiled=True)
+    )(slab, low, high, plane_forward, grad_blocks)
+
+    both = lax.all_to_all(both, SPREAD, 0, 0, tiled=True)
     span = (peers + 6) * width
     back_pencil, depth_term = call(
         depth_kernel,
-        "depth",
-        (shape(act_pencil.shape, bf16), shape((width, 8 * width), f32)),
+        (shape(blocks, bf16), shape((width, 8 * width), f32)),
         (
             pltpu.VMEM((span, slabs * LANES), bf16),
             pltpu.VMEM((span, slabs * LANES), bf16),
             pltpu.VMEM((2 * width, 8 * width), f32),
         ),
         flops=3 * depth_flops,
-    )(act_pencil, grad_pencil, depth_forward, depth_backward)
+    )(both, depth_forward, depth_backward)
     back = lax.all_to_all(back_pencil, SPREAD, 0, 0, tiled=True)
 
     pre_grad, packed = call(
         plane_grad_kernel,
-        "plane_grad",
         (shape((slabs, rows, width, cols), bf16), shape((8, width, 2 * width), f32)),
         (pltpu.VMEM((3 * width, 3 * width), f32),),
         flops=plane_flops,
     )(back, slope, rimmed, depth_term)
     low, high = halo_rows(pre_grad[:, 0], pre_grad[:, rows - 1], "narrow")
-    total = group_total(packed)
+    pieces = spread_pieces(packed)
+    pieces, plane_backward = lax.optimization_barrier((pieces, plane_backward))
+    pieces = lax.all_to_all(copies_of(pieces, group_size(TALL)), TALL, 0, 0, tiled=True)
     (volume_grad,) = call(
         plane_backward_kernel,
-        "plane_backward",
         (shape((slabs, rows, width, cols), bf16),),
         (pltpu.VMEM((slabs, (rows + 2) * width, cols), bf16),),
         flops=plane_flops,
     )(pre_grad, low, high, grad_blocks, plane_backward)
+    volume_grad = volume_grad.transpose(2, 0, 1, 3)
+    pieces, volume_grad = lax.optimization_barrier((pieces, volume_grad))
+    total = lax.all_to_all(copies_of(pieces, group_size(FLAT)), FLAT, 0, 0, tiled=True)
     plane_total, depth_total = call(
         functools.partial(unpack_kernel, gradient_scale),
-        "unpack",
         (shape((9, width, width), f32), shape((7, width, width), f32)),
-    )(total)
-    return volume_grad.transpose(2, 0, 1, 3), plane_total, depth_total
+    )(total.reshape(packed.shape))
+    return volume_grad, plane_total, depth_total
 
 
 def solution(mesh):

time: 157 us -> 136 us (0.87)
  Pallas kernels: 26.5 us -> 10.5 us
  starting transfers between devices: 41.1 us -> 28.9 us
  blocking collectives: 46.2 us -> 53.3 us
  waiting for transfers between devices: 23.3 us -> 28.1 us
  local copies, waits for them, and re-layouts: 16.1 us -> 11.6 us
    pallas_call x5, Pallas kernels: 26.5 us -> 10.5 us  [run(): pl.pallas_call(kernel, out_shape=outs, in_specs=[vmem] * len(args), out_s...]
    all_to_all x3, starting transfers between devices: 28.8 us -> 16.4 us  [the longest x1 6.1 us: spread_pieces(): return lax.all_to_all(pieces, FLAT, 0, 0, tiled=True)]
    ppermute x2, waiting for transfers between devices: 7.46 us -> 13.7 us  [halo_rows(): lax.ppermute(first, axis, backward)]
    all_to_all x2 -> x1, blocking collectives: 27.5 us -> 33.7 us  [on_device(): both = lax.all_to_all(both, SPREAD, 0, 0, tiled=True)]
    unnamed x24 -> x20, local copies, waits for them, and re-layouts: 7.3 us -> 3.44 us
    ppermute x2, waiting for transfers between devices: 5.81 us -> 3.23 us  [halo_rows(): lax.ppermute(last, axis, forward)]
    reshape x1, local copies, waits for them, and re-layouts: 2.96 us -> 0.68 us  [on_device(): grad_blocks = out_grad.reshape(width, slabs, rows, tiles, LANES)]
  transfers between devices with their start and end apart: 7 -> 7, of which waited for: 4 -> 5; matrix products, arithmetic and copies ran while one was open for 5% -> 6% of each run, Pallas kernels for 7% -> 1%
where the time goes in v2:
time: 136 us; the launch traced here: 133 us
  blocking collectives  53.3 us (39%)
  starting transfers between devices  28.9 us (21%)
  waiting for transfers between devices  28.1 us (21%)
  local copies, waits for them, and re-layouts  11.6 us (9%)
  Pallas kernels  10.5 us (8%)
    all_to_all x1, blocking collectives, on_device(): both = lax.all_to_all(both, SPREAD, 0, 0, tiled=True)  33.7 us
    all_to_all x1, blocking collectives, on_device(): back = lax.all_to_all(back_pencil, SPREAD, 0, 0, tiled=True)  19.6 us
    ppermute x2, waiting for transfers between devices, halo_rows(): lax.ppermute(first, axis, backward)  13.7 us
    pallas_call x5, Pallas kernels, run(): pl.pallas_call(kernel, out_shape=outs, in_specs=[vmem] * len(args), out_s...  10.5 us
    ppermute x2, starting transfers between devices, halo_rows(): lax.ppermute(last, axis, forward)  9.9 us
    all_to_all x1, starting transfers between devices, spread_pieces(): return lax.all_to_all(pieces, FLAT, 0, 0, tiled=True)  6.1 us
    all_to_all x1, waiting for transfers between devices, spread_pieces(): return lax.all_to_all(pieces, FLAT, 0, 0, tiled=True)  5.7 us
    all_to_all x1, waiting for transfers between devices, on_device(): lax.all_to_all(copies_of(pieces, group_size(FLAT)), FLAT, 0, 0, tiled=True)  5.44 us
  transfers between devices with their start and end apart: 7, of which 5 were waited for; matrix products, arithmetic and copies ran while one was open for 6% of the time, Pallas kernels for 1%

profile of v2, /device:TPU:2, one launch (start us, length us, event | category | flops | bytes accessed | tf_op | source)
XLA Modules:
  0.0 133.4 jit_solution(3176973892861236675)
XLA Ops:
  0.7 1.8 %copy.38 = bf16[64,2,8,512]{3,0,1,2:T(8,128)(2,1)S(1)} copy(bf16[64,2,8,512]{3,2,1,0:T(8,128)(2,1)} %param.4) | data formatting | bytes 2097152 | tf_op args[0]
  2.5 0.7 slice_bitcast_fusion.2
  3.2 5.2 %collective-permute-start = (bf16[2,64,512]{2,1,0:T(8,128)(2,1)}, bf16[2,64,512]{2,1,0:T(8,128)(2,1)S(1)}, u32[]{:S(2)}, u32[]{:S(2)}) collective-permute-start(bf16[2,64,512]{2,1,0:T(8,128)(2,1)} %get-tuple-element.48), channel_id=1, source_target_pairs={{0,1},{1,2},{2,3},{4,5},{5,6},{6,7},{8,9},{9,10},{10,11},{12,13},{... | collective-permute-start | bytes 393224 | tf_op jit(solution)/shard_map/ppermute | solution.py:29
  8.4 1.3 collective-permute-start.1
  9.9 0.8 reshape.43
  10.8 0.8 reshape.44
  11.6 0.7 copy.32
  12.3 0.7 copy.33
  13.4 0.7 copy.25
  14.1 0.6 copy.26.vol_ref
  14.7 6.3 %collective-permute-done.1.high_ref = bf16[2,64,512]{2,1,0:T(8,128)(2,1)S(1)} collective-permute-done((bf16[2,64,512]{2,1,0:T(8,128)(2,1)}, bf16[2,64,512]{2,1,0:T(8,128)(2,1)S(1)}, u32[]{:S(2)}, u32[]{:S(2)}) %collective-permute-start.1) | collective-permute-done | bytes 131104 | tf_op jit(solution)/shard_map/ppermute | solution.py:29
  21.0 1.9 %shard_map.67 = (bf16[32,4,64,128]{3,2,1,0:T(8,128)(2,1)S(1)}, f32[2,8,64,512]{3,2,1,0:T(8,128)S(1)}, bf16[2,640,512]{2,1,0:T(8,128)(2,1)S(1)}) custom-call(bf16[2,8,64,512]{3,2,1,0:T(8,128)(2,1)S(1)} %copy.26.vol_ref, bf16[2,64,512]{2,1,0:T(8,128)(2,1)S(1)} %collective-permute-done.low_ref, bf16[2,64,512]{2,1,0:T(8,128)(2,1)S(1)} %collective-permute-done.1.high_ref, ...), custom_call_target="tpu_custom_call" | custom-call | flops 603979776 | bytes 7938048 | tf_op jit(solution)/shard_map/pallas_call | solution.py:210
  22.9 33.7 %all_to_all.25.both_ref = bf16[32,4,64,128]{3,2,1,0:T(8,128)(2,1)S(1)} all-to-all(bf16[32,4,64,128]{3,2,1,0:T(8,128)(2,1)S(1)} %get-tuple-element.24), channel_id=1, replica_groups=mesh['wide_0'=4,'wide_1'=4,'wide_2'=2,'wide_3'=2,'narrow'=4] {'wide_0','..., dimensions={0} | all-to-all | bytes 4194304 | tf_op jit(solution)/shard_map/all_to_all | solution.py:280
  56.6 3.8 %shard_map.68 = (bf16[32,2,64,128]{3,2,1,0:T(8,128)(2,1)S(1)}, f32[64,512]{1,0:T(8,128)S(1)}) custom-call(bf16[32,4,64,128]{3,2,1,0:T(8,128)(2,1)S(1)} %all_to_all.25.both_ref, bf16[128,512]{1,0:T(8,128)(2,1)S(1)} %get-tuple-element.25.wf_ref, bf16[128,512]{1,0:T(8,128)(2,1)S(1)} %get-tuple-element.26.wb_ref), custom_call_target="tpu_custom_call" | custom-call | flops 1409286144 | bytes 3538944 | tf_op jit(solution)/shard_map/pallas_call | solution.py:210
  60.4 19.6 %all_to_all.26.back_ref = bf16[32,2,64,128]{3,2,1,0:T(8,128)(2,1)S(1)} all-to-all(bf16[32,2,64,128]{3,2,1,0:T(8,128)(2,1)S(1)} %get-tuple-element.27), channel_id=1, replica_groups=mesh['wide_0'=4,'wide_1'=4,'wide_2'=2,'wide_3'=2,'narrow'=4] {'wide_0','..., dimensions={0} | all-to-all | bytes 2097152 | tf_op jit(solution)/shard_map/all_to_all | solution.py:292
  80.0 2.3 %shard_map.69 = (bf16[2,8,64,512]{3,2,1,0:T(8,128)(2,1)S(1)}, f32[8,64,128]{2,1,0:T(8,128)}) custom-call(bf16[32,2,64,128]{3,2,1,0:T(8,128)(2,1)S(1)} %all_to_all.26.back_ref, f32[2,8,64,512]{3,2,1,0:T(8,128)S(1)} %get-tuple-element.28.slope_ref, bf16[2,640,512]{2,1,0:T(8,128)(2,1)S(1)} %get-tuple-element.29.rows_ref, f32[64,512]{1,0:T(8,128)S(1)} %get-tuple-element.30.dwz_ref), custom_call_target="tpu_custom_call" | custom-call | flops 603979776 | bytes 5898240 | tf_op jit(solution)/shard_map/pallas_call | solution.py:210
  82.3 6.1 %all-to-all-start.2 = ((f32[16,32,128]{2,1,0:T(8,128)}), f32[16,32,128]{2,1,0:T(8,128)S(1)}, u32[]{:S(2)}, u32[]{:S(2)}) async-start(f32[16,32,128]{2,1,0:T(8,128)} %bitcast.16), calls=%async_computation.2 | async-start | bytes 524288 | tf_op jit(solution)/shard_map/all_to_all | solution.py:225
  88.4 0.2 copy.27
  88.6 0.8 rev.7
  89.5 5.7 %all-to-all-done.2 = f32[16,32,128]{2,1,0:T(8,128)S(1)} async-done(((f32[16,32,128]{2,1,0:T(8,128)}), f32[16,32,128]{2,1,0:T(8,128)S(1)}, u32[]{:S(2)}, u32[]{:S(2)}) %all-to-all-start.2) | async-done | bytes 262176 | tf_op jit(solution)/shard_map/all_to_all | solution.py:225
  95.3 0.7 broadcast_in_dim.4
  96.0 5.0 %all-to-all-start.3 = ((f32[16,32,128]{2,1,0:T(8,128)}), f32[16,32,128]{2,1,0:T(8,128)S(1)}, u32[]{:S(2)}, u32[]{:S(2)}) async-start(f32[16,32,128]{2,1,0:T(8,128)} %broadcast_in_dim.4), calls=%async_computation.3 | async-start | bytes 524288 | tf_op jit(solution)/shard_map/all_to_all | solution.py:303
  101.0 4.7 %collective-permute-start.2 = (bf16[2,64,512]{2,1,0:T(8,128)(2,1)S(1)}, bf16[2,64,512]{2,1,0:T(8,128)(2,1)S(1)}, u32[]{:S(2)}, u32[]{:S(2)}) collective-permute-start(bf16[2,64,512]{2,1,0:T(8,128)(2,1)S(1)} %get-tuple-element.46), channel_id=1, source_target_pairs={{0,1},{1,2},{2,3},{4,5},{5,6},{6,7},{8,9},{9,10},{10,11},{12,13},{... | collective-permute-start | bytes 393224 | tf_op jit(solution)/shard_map/ppermute | solution.py:29
  105.8 1.3 collective-permute-start.3
  107.1 3.2 %collective-permute-done.2.low_ref = bf16[2,64,512]{2,1,0:T(8,128)(2,1)S(1)} collective-permute-done((bf16[2,64,512]{2,1,0:T(8,128)(2,1)S(1)}, bf16[2,64,512]{2,1,0:T(8,128)(2,1)S(1)}, u32[]{:S(2)}, u32[]{:S(2)}) %collective-permute-start.2) | collective-permute-done | bytes 131104 | tf_op jit(solution)/shard_map/ppermute | solution.py:29
  110.3 7.4 %collective-permute-done.3.high_ref = bf16[2,64,512]{2,1,0:T(8,128)(2,1)S(1)} collective-permute-done((bf16[2,64,512]{2,1,0:T(8,128)(2,1)S(1)}, bf16[2,64,512]{2,1,0:T(8,128)(2,1)S(1)}, u32[]{:S(2)}, u32[]{:S(2)}) %collective-permute-start.3) | collective-permute-done | bytes 131104 | tf_op jit(solution)/shard_map/ppermute | solution.py:29
  117.7 1.7 %shard_map.70 = bf16[2,8,64,512]{3,2,1,0:T(8,128)(2,1)S(1)} custom-call(bf16[2,8,64,512]{3,2,1,0:T(8,128)(2,1)S(1)} %get-tuple-element.33.pre_ref, bf16[2,64,512]{2,1,0:T(8,128)(2,1)S(1)} %collective-permute-done.2.low_ref, bf16[2,64,512]{2,1,0:T(8,128)(2,1)S(1)} %collective-permute-done.3.high_ref, bf16[32,2,64,128]{3,2,1,0:T(8,128)(2,1)S(1)} %bitcast.37, ...), custom_call_target="tpu_custom_call" | custom-call | flops 603979776 | bytes 3481600 | tf_op jit(solution)/shard_map/pallas_call | solution.py:210
  119.4 0.7 broadcast_in_dim.5
  120.2 5.3 %all-to-all-start.4 = ((f32[16,32,128]{2,1,0:T(8,128)}), f32[16,32,128]{2,1,0:T(8,128)S(1)}, u32[]{:S(2)}, u32[]{:S(2)}) async-start(f32[16,32,128]{2,1,0:T(8,128)} %broadcast_in_dim.5), calls=%async_computation.4 | async-start | bytes 524288 | tf_op jit(solution)/shard_map/all_to_all | solution.py:312
  125.5 1.5 %copy.30 = bf16[64,2,8,512]{3,2,1,0:T(8,128)(2,1)} copy(bf16[64,2,8,512]{3,0,2,1:T(8,128)(2,1)S(1)} %bitcast.38) | data formatting | bytes 2097152
  127.1 5.4 %all-to-all-done.4 = f32[16,32,128]{2,1,0:T(8,128)S(1)} async-done(((f32[16,32,128]{2,1,0:T(8,128)}), f32[16,32,128]{2,1,0:T(8,128)S(1)}, u32[]{:S(2)}, u32[]{:S(2)}) %all-to-all-start.4) | async-done | bytes 262176 | tf_op jit(solution)/shard_map/all_to_all | solution.py:312
  132.5 0.9 shard_map.71
  (32 shorter events, 0.9 us)
Async XLA Ops:
  0.6 9.1 %copy-start.4 = (bf16[7,64,64]{2,1,0:T(8,128)(2,1)S(1)}, bf16[7,64,64]{2,1,0:T(8,128)(2,1)}, u32[]{:S(2)}) copy-start(bf16[7,64,64]{2,1,0:T(8,128)(2,1)} %param.7) | copy-start | bytes 172036
  0.6 12.4 %copy-start.2 = (bf16[9,64,64]{2,1,0:T(8,128)(2,1)S(1)}, bf16[9,64,64]{2,1,0:T(8,128)(2,1)}, u32[]{:S(2)}) copy-start(bf16[9,64,64]{2,1,0:T(8,128)(2,1)} %param.6) | copy-start | bytes 221188
  2.5 10.8 %copy-start.1 = (bf16[64,2,8,512]{3,2,1,0:T(8,128)(2,1)S(1)}, bf16[64,2,8,512]{3,2,1,0:T(8,128)(2,1)}, u32[]{:S(2)}) copy-start(bf16[64,2,8,512]{3,2,1,0:T(8,128)(2,1)} %param.5) | copy-start | bytes 3145732
  3.2 11.5 %collective-permute-start = (bf16[2,64,512]{2,1,0:T(8,128)(2,1)}, bf16[2,64,512]{2,1,0:T(8,128)(2,1)S(1)}, u32[]{:S(2)}, u32[]{:S(2)}) collective-permute-start(bf16[2,64,512]{2,1,0:T(8,128)(2,1)} %get-tuple-element.48), channel_id=1, source_target_pairs={{0,1},{1,2},{2,3},{4,5},{5,6},{6,7},{8,9},{9,10},{10,11},{12,13},{... | collective-permute-start | bytes 393224 | tf_op jit(solution)/shard_map/ppermute | solution.py:29
  8.4 12.6 %collective-permute-start.1 = (bf16[2,64,512]{2,1,0:T(8,128)(2,1)}, bf16[2,64,512]{2,1,0:T(8,128)(2,1)S(1)}, u32[]{:S(2)}, u32[]{:S(2)}) collective-permute-start(bf16[2,64,512]{2,1,0:T(8,128)(2,1)} %get-tuple-element.47), channel_id=1, source_target_pairs={{1,0},{2,1},{3,2},{5,4},{6,5},{7,6},{9,8},{10,9},{11,10},{13,12},{... | collective-permute-start | bytes 393224 | tf_op jit(solution)/shard_map/ppermute | solution.py:29
  9.8 4.2 %copy-start = (bf16[64,2,8,512]{3,2,1,0:T(8,128)(2,1)S(1)}, bf16[64,2,8,512]{3,2,1,0:T(8,128)(2,1)}, u32[]{:S(2)}) copy-start(bf16[64,2,8,512]{3,2,1,0:T(8,128)(2,1)} %param.4) | copy-start | bytes 3145732
  13.3 1.3 copy-start.5
  13.3 1.3 copy-start.6
  13.4 1.3 copy-start.7
  13.4 1.3 copy-start.8
  80.0 8.4 %copy-start.3 = (bf16[9,64,64]{2,1,0:T(8,128)(2,1)S(1)}, bf16[9,64,64]{2,1,0:T(8,128)(2,1)}, u32[]{:S(2)}) copy-start(bf16[9,64,64]{2,1,0:T(8,128)(2,1)} %param.6) | copy-start | bytes 221188
  82.3 13.0 %all-to-all-start.2 = ((f32[16,32,128]{2,1,0:T(8,128)}), f32[16,32,128]{2,1,0:T(8,128)S(1)}, u32[]{:S(2)}, u32[]{:S(2)}) async-start(f32[16,32,128]{2,1,0:T(8,128)} %bitcast.16), calls=%async_computation.2 | async-start | bytes 524288 | tf_op jit(solution)/shard_map/all_to_all | solution.py:225
  96.0 23.4 %all-to-all-start.3 = ((f32[16,32,128]{2,1,0:T(8,128)}), f32[16,32,128]{2,1,0:T(8,128)S(1)}, u32[]{:S(2)}, u32[]{:S(2)}) async-start(f32[16,32,128]{2,1,0:T(8,128)} %broadcast_in_dim.4), calls=%async_computation.3 | async-start | bytes 524288 | tf_op jit(solution)/shard_map/all_to_all | solution.py:303
  101.0 9.3 %collective-permute-start.2 = (bf16[2,64,512]{2,1,0:T(8,128)(2,1)S(1)}, bf16[2,64,512]{2,1,0:T(8,128)(2,1)S(1)}, u32[]{:S(2)}, u32[]{:S(2)}) collective-permute-start(bf16[2,64,512]{2,1,0:T(8,128)(2,1)S(1)} %get-tuple-element.46), channel_id=1, source_target_pairs={{0,1},{1,2},{2,3},{4,5},{5,6},{6,7},{8,9},{9,10},{10,11},{12,13},{... | collective-permute-start | bytes 393224 | tf_op jit(solution)/shard_map/ppermute | solution.py:29
  105.8 12.0 %collective-permute-start.3 = (bf16[2,64,512]{2,1,0:T(8,128)(2,1)S(1)}, bf16[2,64,512]{2,1,0:T(8,128)(2,1)S(1)}, u32[]{:S(2)}, u32[]{:S(2)}) collective-permute-start(bf16[2,64,512]{2,1,0:T(8,128)(2,1)S(1)} %get-tuple-element.45), channel_id=1, source_target_pairs={{1,0},{2,1},{3,2},{5,4},{6,5},{7,6},{9,8},{10,9},{11,10},{13,12},{... | collective-permute-start | bytes 393224 | tf_op jit(solution)/shard_map/ppermute | solution.py:29
  120.2 12.3 %all-to-all-start.4 = ((f32[16,32,128]{2,1,0:T(8,128)}), f32[16,32,128]{2,1,0:T(8,128)S(1)}, u32[]{:S(2)}, u32[]{:S(2)}) async-start(f32[16,32,128]{2,1,0:T(8,128)} %broadcast_in_dim.5), calls=%async_computation.4 | async-start | bytes 524288 | tf_op jit(solution)/shard_map/all_to_all | solution.py:312

commit v3 on v2

--- a/solution.py
+++ b/solution.py
@@ -220,14 +220,22 @@
     return run
 
 
+def copies_kernel(pieces_ref, copies_ref):
+    part = pieces_ref[0]
+    for i in range(1, pieces_ref.shape[0]):
+        part = part + pieces_ref[i]
+    for i in range(copies_ref.shape[0]):
+        copies_ref[i] = part
+
+
 def spread_pieces(packed):
-    pieces = packed.reshape(group_size(FLAT), -1, LANES)
-    return lax.all_to_all(pieces, FLAT, 0, 0, tiled=True)
+    pieces = packed.reshape(group_size(TALL), -1, LANES)
+    return lax.all_to_all(pieces, TALL, 0, 0, tiled=True)
 
 
 def copies_of(pieces, count):
-    part = jnp.sum(pieces, axis=0)
-    return jnp.broadcast_to(part[None], (count, *part.shape))
+    shape = jax.ShapeDtypeStruct((count, *pieces.shape[1:]), pieces.dtype)
+    return call(copies_kernel, (shape,))(pieces)[0]
 
 
 def on_device(volume, out_grad, plane_kernel, z_axis_kernel):
@@ -299,8 +307,8 @@
     )(back, slope, rimmed, depth_term)
     low, high = halo_rows(pre_grad[:, 0], pre_grad[:, rows - 1], "narrow")
     pieces = spread_pieces(packed)
+    pieces = lax.all_to_all(copies_of(pieces, group_size(FLAT)), FLAT, 0, 0, tiled=True)
     pieces, plane_backward = lax.optimization_barrier((pieces, plane_backward))
-    pieces = lax.all_to_all(copies_of(pieces, group_size(TALL)), TALL, 0, 0, tiled=True)
     (volume_grad,) = call(
         plane_backward_kernel,
         (shape((slabs, rows, width, cols), bf16),),
@@ -308,8 +316,7 @@
         flops=plane_flops,
     )(pre_grad, low, high, grad_blocks, plane_backward)
     volume_grad = volume_grad.transpose(2, 0, 1, 3)
-    pieces, volume_grad = lax.optimization_barrier((pieces, volume_grad))
-    total = lax.all_to_all(copies_of(pieces, group_size(FLAT)), FLAT, 0, 0, tiled=True)
+    total = lax.all_to_all(copies_of(pieces, group_size(TALL)), TALL, 0, 0, tiled=True)
     plane_total, depth_total = call(
         functools.partial(unpack_kernel, gradient_scale),
         (shape((9, width, width), f32), shape((7, width, width), f32)),

time: 136 us -> 139 us (1.022)
  blocking collectives: 53.3 us -> 69.2 us
  starting transfers between devices: 28.9 us -> 22.2 us
  waiting for transfers between devices: 28.1 us -> 22.9 us
  local copies, waits for them, and re-layouts: 11.6 us -> 10.1 us
    all_to_all x0 -> x1, blocking collectives: none -> 15.9 us  [spread_pieces(): return lax.all_to_all(pieces, TALL, 0, 0, tiled=True)]
    all_to_all x1 -> x0, starting transfers between devices: 6.1 us -> none  [spread_pieces(): return lax.all_to_all(pieces, FLAT, 0, 0, tiled=True)]
    all_to_all x1 -> x0, waiting for transfers between devices: 5.7 us -> none  [spread_pieces(): return lax.all_to_all(pieces, FLAT, 0, 0, tiled=True)]
    broadcast_in_dim x2 -> x0, local copies, waits for them, and re-layouts: 1.46 us -> none  [copies_of(): return jnp.broadcast_to(part[None], (count, *part.shape))]
    pallas_call x5 -> x7, Pallas kernels: 10.5 us -> 11.3 us  [run(): pl.pallas_call(kernel, out_shape=outs, in_specs=[vmem] * len(args), out_s...]
  transfers between devices with their start and end apart: 7 -> 6, of which waited for: 5 -> 4; matrix products, arithmetic and copies ran while one was open for 6% -> 6% of each run, Pallas kernels for 1% -> 1%
where the time goes in v3:
time: 139 us; the launch traced here: 137 us
  blocking collectives  69.2 us (50%)
  waiting for transfers between devices  22.9 us (16%)
  starting transfers between devices  22.2 us (16%)
  Pallas kernels  11.3 us (8%)
  local copies, waits for them, and re-layouts  10.1 us (7%)
    all_to_all x1, blocking collectives, on_device(): both = lax.all_to_all(both, SPREAD, 0, 0, tiled=True)  33.7 us
    all_to_all x1, blocking collectives, on_device(): back = lax.all_to_all(back_pencil, SPREAD, 0, 0, tiled=True)  19.6 us
    all_to_all x1, blocking collectives, spread_pieces(): return lax.all_to_all(pieces, TALL, 0, 0, tiled=True)  15.9 us
    ppermute x2, waiting for transfers between devices, halo_rows(): lax.ppermute(first, axis, backward)  13.7 us
    pallas_call x7, Pallas kernels, run(): pl.pallas_call(kernel, out_shape=outs, in_specs=[vmem] * len(args), out_s...  11.3 us
    ppermute x2, starting transfers between devices, halo_rows(): lax.ppermute(last, axis, forward)  9.9 us
    all_to_all x1, waiting for transfers between devices, on_device(): lax.all_to_all(copies_of(pieces, group_size(FLAT)), FLAT, 0, 0, tiled=True)  5.97 us
    all_to_all x1, starting transfers between devices, on_device(): lax.all_to_all(copies_of(pieces, group_size(FLAT)), FLAT, 0, 0, tiled=True)  5.07 us
  transfers between devices with their start and end apart: 6, of which 4 were waited for; matrix products, arithmetic and copies ran while one was open for 6% of the time, Pallas kernels for 1%

profile of v3, /device:TPU:2, one launch (start us, length us, event | category | flops | bytes accessed | tf_op | source)
XLA Modules:
  0.0 136.7 jit_solution(5917877915462821336)
XLA Ops:
  0.7 1.8 %copy.38 = bf16[64,2,8,512]{3,0,1,2:T(8,128)(2,1)S(1)} copy(bf16[64,2,8,512]{3,2,1,0:T(8,128)(2,1)} %param.4) | data formatting | bytes 2097152 | tf_op args[0]
  2.5 0.7 slice_bitcast_fusion.2
  3.2 5.2 %collective-permute-start = (bf16[2,64,512]{2,1,0:T(8,128)(2,1)}, bf16[2,64,512]{2,1,0:T(8,128)(2,1)S(1)}, u32[]{:S(2)}, u32[]{:S(2)}) collective-permute-start(bf16[2,64,512]{2,1,0:T(8,128)(2,1)} %get-tuple-element.44), channel_id=1, source_target_pairs={{0,1},{1,2},{2,3},{4,5},{5,6},{6,7},{8,9},{9,10},{10,11},{12,13},{... | collective-permute-start | bytes 393224 | tf_op jit(solution)/shard_map/ppermute | solution.py:29
  8.4 1.3 collective-permute-start.1
  9.9 0.8 reshape.41
  10.8 0.8 reshape.42
  11.6 0.7 copy.32
  12.3 0.7 copy.33
  13.1 0.2 reshape.40.w_ref
  13.3 0.7 copy.25
  14.0 0.6 copy.26.vol_ref
  14.7 6.3 %collective-permute-done.1.high_ref = bf16[2,64,512]{2,1,0:T(8,128)(2,1)S(1)} collective-permute-done((bf16[2,64,512]{2,1,0:T(8,128)(2,1)}, bf16[2,64,512]{2,1,0:T(8,128)(2,1)S(1)}, u32[]{:S(2)}, u32[]{:S(2)}) %collective-permute-start.1) | collective-permute-done | bytes 131104 | tf_op jit(solution)/shard_map/ppermute | solution.py:29
  21.0 1.9 %shard_map.67 = (bf16[32,4,64,128]{3,2,1,0:T(8,128)(2,1)S(1)}, f32[2,8,64,512]{3,2,1,0:T(8,128)S(1)}, bf16[2,640,512]{2,1,0:T(8,128)(2,1)S(1)}) custom-call(bf16[2,8,64,512]{3,2,1,0:T(8,128)(2,1)S(1)} %copy.26.vol_ref, bf16[2,64,512]{2,1,0:T(8,128)(2,1)S(1)} %collective-permute-done.low_ref, bf16[2,64,512]{2,1,0:T(8,128)(2,1)S(1)} %collective-permute-done.1.high_ref, ...), custom_call_target="tpu_custom_call" | custom-call | flops 603979776 | bytes 7938048 | tf_op jit(solution)/shard_map/pallas_call | solution.py:210
  22.9 33.7 %all_to_all.25.both_ref = bf16[32,4,64,128]{3,2,1,0:T(8,128)(2,1)S(1)} all-to-all(bf16[32,4,64,128]{3,2,1,0:T(8,128)(2,1)S(1)} %get-tuple-element.22), channel_id=1, replica_groups=mesh['wide_0'=4,'wide_1'=4,'wide_2'=2,'wide_3'=2,'narrow'=4] {'wide_0','..., dimensions={0} | all-to-all | bytes 4194304 | tf_op jit(solution)/shard_map/all_to_all | solution.py:288
  56.6 3.8 %shard_map.68 = (bf16[32,2,64,128]{3,2,1,0:T(8,128)(2,1)S(1)}, f32[64,512]{1,0:T(8,128)S(1)}) custom-call(bf16[32,4,64,128]{3,2,1,0:T(8,128)(2,1)S(1)} %all_to_all.25.both_ref, bf16[128,512]{1,0:T(8,128)(2,1)S(1)} %get-tuple-element.23.wf_ref, bf16[128,512]{1,0:T(8,128)(2,1)S(1)} %get-tuple-element.24.wb_ref), custom_call_target="tpu_custom_call" | custom-call | flops 1409286144 | bytes 3538944 | tf_op jit(solution)/shard_map/pallas_call | solution.py:210
  60.4 19.6 %all_to_all.26.back_ref = bf16[32,2,64,128]{3,2,1,0:T(8,128)(2,1)S(1)} all-to-all(bf16[32,2,64,128]{3,2,1,0:T(8,128)(2,1)S(1)} %get-tuple-element.25), channel_id=1, replica_groups=mesh['wide_0'=4,'wide_1'=4,'wide_2'=2,'wide_3'=2,'narrow'=4] {'wide_0','..., dimensions={0} | all-to-all | bytes 2097152 | tf_op jit(solution)/shard_map/all_to_all | solution.py:300
  80.0 1.6 %shard_map.69 = (bf16[2,8,64,512]{3,2,1,0:T(8,128)(2,1)S(1)}, f32[8,64,128]{2,1,0:T(8,128)S(1)}) custom-call(bf16[32,2,64,128]{3,2,1,0:T(8,128)(2,1)S(1)} %all_to_all.26.back_ref, f32[2,8,64,512]{3,2,1,0:T(8,128)S(1)} %get-tuple-element.26.slope_ref, bf16[2,640,512]{2,1,0:T(8,128)(2,1)S(1)} %get-tuple-element.27.rows_ref, ...), custom_call_target="tpu_custom_call" | custom-call | flops 603979776 | bytes 5898240 | tf_op jit(solution)/shard_map/pallas_call | solution.py:210
  81.6 15.9 %all_to_all.27.pieces_ref = f32[16,32,128]{2,1,0:T(8,128)S(1)} all-to-all(f32[16,32,128]{2,1,0:T(8,128)S(1)} %bitcast.40), channel_id=1, replica_groups=mesh['wide_0'=4,'wide_1'=4,'wide_2'=2,'wide_3'=2,'narrow'=4] {'wide_2','..., dimensions={0} | all-to-all | bytes 524288 | tf_op jit(solution)/shard_map/all_to_all | solution.py:233
  97.5 0.7 shard_map.70
  98.2 5.1 %all-to-all-start.3 = ((f32[16,32,128]{2,1,0:T(8,128)}), f32[16,32,128]{2,1,0:T(8,128)S(1)}, u32[]{:S(2)}, u32[]{:S(2)}) async-start(f32[16,32,128]{2,1,0:T(8,128)} %shard_map.70), calls=%async_computation.3 | async-start | bytes 524288 | tf_op jit(solution)/shard_map/all_to_all | solution.py:310
  103.3 0.2 copy.29
  103.5 0.8 rev.7
  104.5 6.0 %all-to-all-done.3.pieces_ref = f32[16,32,128]{2,1,0:T(8,128)S(1)} async-done(((f32[16,32,128]{2,1,0:T(8,128)}), f32[16,32,128]{2,1,0:T(8,128)S(1)}, u32[]{:S(2)}, u32[]{:S(2)}) %all-to-all-start.3) | async-done | bytes 262176 | tf_op jit(solution)/shard_map/all_to_all | solution.py:310
  110.4 0.7 shard_map.72
  111.2 4.6 %all-to-all-start.4 = ((f32[16,32,128]{2,1,0:T(8,128)}), f32[16,32,128]{2,1,0:T(8,128)S(1)}, u32[]{:S(2)}, u32[]{:S(2)}) async-start(f32[16,32,128]{2,1,0:T(8,128)} %shard_map.72), calls=%async_computation.4 | async-start | bytes 524288 | tf_op jit(solution)/shard_map/all_to_all | solution.py:319
  115.9 4.7 %collective-permute-start.2 = (bf16[2,64,512]{2,1,0:T(8,128)(2,1)S(1)}, bf16[2,64,512]{2,1,0:T(8,128)(2,1)S(1)}, u32[]{:S(2)}, u32[]{:S(2)}) collective-permute-start(bf16[2,64,512]{2,1,0:T(8,128)(2,1)S(1)} %get-tuple-element.42), channel_id=1, source_target_pairs={{0,1},{1,2},{2,3},{4,5},{5,6},{6,7},{8,9},{9,10},{10,11},{12,13},{... | collective-permute-start | bytes 393224 | tf_op jit(solution)/shard_map/ppermute | solution.py:29
  120.6 1.3 collective-permute-start.3
  121.9 3.2 %collective-permute-done.2.low_ref = bf16[2,64,512]{2,1,0:T(8,128)(2,1)S(1)} collective-permute-done((bf16[2,64,512]{2,1,0:T(8,128)(2,1)S(1)}, bf16[2,64,512]{2,1,0:T(8,128)(2,1)S(1)}, u32[]{:S(2)}, u32[]{:S(2)}) %collective-permute-start.2) | collective-permute-done | bytes 131104 | tf_op jit(solution)/shard_map/ppermute | solution.py:29
  125.1 7.4 %collective-permute-done.3.high_ref = bf16[2,64,512]{2,1,0:T(8,128)(2,1)S(1)} collective-permute-done((bf16[2,64,512]{2,1,0:T(8,128)(2,1)S(1)}, bf16[2,64,512]{2,1,0:T(8,128)(2,1)S(1)}, u32[]{:S(2)}, u32[]{:S(2)}) %collective-permute-start.3) | collective-permute-done | bytes 131104 | tf_op jit(solution)/shard_map/ppermute | solution.py:29
  132.6 1.7 %shard_map.71 = bf16[2,8,64,512]{3,2,1,0:T(8,128)(2,1)S(1)} custom-call(bf16[2,8,64,512]{3,2,1,0:T(8,128)(2,1)S(1)} %get-tuple-element.29.pre_ref, bf16[2,64,512]{2,1,0:T(8,128)(2,1)S(1)} %collective-permute-done.2.low_ref, bf16[2,64,512]{2,1,0:T(8,128)(2,1)S(1)} %collective-permute-done.3.high_ref, bf16[32,2,64,128]{3,2,1,0:T(8,128)(2,1)S(1)} %bitcast.37, ...), custom_call_target="tpu_custom_call" | custom-call | flops 603979776 | bytes 3481600 | tf_op jit(solution)/shard_map/pallas_call | solution.py:210
  134.3 1.5 %copy.30 = bf16[64,2,8,512]{3,2,1,0:T(8,128)(2,1)} copy(bf16[64,2,8,512]{3,0,2,1:T(8,128)(2,1)S(1)} %bitcast.38) | data formatting | bytes 2097152
  135.8 0.9 shard_map.73
  (29 shorter events, 0.7 us)
Async XLA Ops:
  0.6 9.1 %copy-start.4 = (bf16[7,64,64]{2,1,0:T(8,128)(2,1)S(1)}, bf16[7,64,64]{2,1,0:T(8,128)(2,1)}, u32[]{:S(2)}) copy-start(bf16[7,64,64]{2,1,0:T(8,128)(2,1)} %param.7) | copy-start | bytes 172036
  0.6 12.4 %copy-start.2 = (bf16[9,64,64]{2,1,0:T(8,128)(2,1)S(1)}, bf16[9,64,64]{2,1,0:T(8,128)(2,1)}, u32[]{:S(2)}) copy-start(bf16[9,64,64]{2,1,0:T(8,128)(2,1)} %param.6) | copy-start | bytes 221188
  2.5 10.8 %copy-start.1 = (bf16[64,2,8,512]{3,2,1,0:T(8,128)(2,1)S(1)}, bf16[64,2,8,512]{3,2,1,0:T(8,128)(2,1)}, u32[]{:S(2)}) copy-start(bf16[64,2,8,512]{3,2,1,0:T(8,128)(2,1)} %param.5) | copy-start | bytes 3145732
  3.2 11.5 %collective-permute-start = (bf16[2,64,512]{2,1,0:T(8,128)(2,1)}, bf16[2,64,512]{2,1,0:T(8,128)(2,1)S(1)}, u32[]{:S(2)}, u32[]{:S(2)}) collective-permute-start(bf16[2,64,512]{2,1,0:T(8,128)(2,1)} %get-tuple-element.44), channel_id=1, source_target_pairs={{0,1},{1,2},{2,3},{4,5},{5,6},{6,7},{8,9},{9,10},{10,11},{12,13},{... | collective-permute-start | bytes 393224 | tf_op jit(solution)/shard_map/ppermute | solution.py:29
  8.4 12.6 %collective-permute-start.1 = (bf16[2,64,512]{2,1,0:T(8,128)(2,1)}, bf16[2,64,512]{2,1,0:T(8,128)(2,1)S(1)}, u32[]{:S(2)}, u32[]{:S(2)}) collective-permute-start(bf16[2,64,512]{2,1,0:T(8,128)(2,1)} %get-tuple-element.43), channel_id=1, source_target_pairs={{1,0},{2,1},{3,2},{5,4},{6,5},{7,6},{9,8},{10,9},{11,10},{13,12},{... | collective-permute-start | bytes 393224 | tf_op jit(solution)/shard_map/ppermute | solution.py:29
  9.8 4.2 %copy-start = (bf16[64,2,8,512]{3,2,1,0:T(8,128)(2,1)S(1)}, bf16[64,2,8,512]{3,2,1,0:T(8,128)(2,1)}, u32[]{:S(2)}) copy-start(bf16[64,2,8,512]{3,2,1,0:T(8,128)(2,1)} %param.4) | copy-start | bytes 3145732
  13.3 1.3 copy-start.5
  13.3 1.3 copy-start.6
  13.3 1.3 copy-start.7
  13.3 1.3 copy-start.8
  80.0 23.3 %copy-start.3 = (bf16[9,64,64]{2,1,0:T(8,128)(2,1)S(1)}, bf16[9,64,64]{2,1,0:T(8,128)(2,1)}, u32[]{:S(2)}) copy-start(bf16[9,64,64]{2,1,0:T(8,128)(2,1)} %param.6) | copy-start | bytes 221188
  98.2 12.2 %all-to-all-start.3 = ((f32[16,32,128]{2,1,0:T(8,128)}), f32[16,32,128]{2,1,0:T(8,128)S(1)}, u32[]{:S(2)}, u32[]{:S(2)}) async-start(f32[16,32,128]{2,1,0:T(8,128)} %shard_map.70), calls=%async_computation.3 | async-start | bytes 524288 | tf_op jit(solution)/shard_map/all_to_all | solution.py:310
  111.2 24.6 %all-to-all-start.4 = ((f32[16,32,128]{2,1,0:T(8,128)}), f32[16,32,128]{2,1,0:T(8,128)S(1)}, u32[]{:S(2)}, u32[]{:S(2)}) async-start(f32[16,32,128]{2,1,0:T(8,128)} %shard_map.72), calls=%async_computation.4 | async-start | bytes 524288 | tf_op jit(solution)/shard_map/all_to_all | solution.py:319
  115.9 9.3 %collective-permute-start.2 = (bf16[2,64,512]{2,1,0:T(8,128)(2,1)S(1)}, bf16[2,64,512]{2,1,0:T(8,128)(2,1)S(1)}, u32[]{:S(2)}, u32[]{:S(2)}) collective-permute-start(bf16[2,64,512]{2,1,0:T(8,128)(2,1)S(1)} %get-tuple-element.42), channel_id=1, source_target_pairs={{0,1},{1,2},{2,3},{4,5},{5,6},{6,7},{8,9},{9,10},{10,11},{12,13},{... | collective-permute-start | bytes 393224 | tf_op jit(solution)/shard_map/ppermute | solution.py:29
  120.6 12.0 %collective-permute-start.3 = (bf16[2,64,512]{2,1,0:T(8,128)(2,1)S(1)}, bf16[2,64,512]{2,1,0:T(8,128)(2,1)S(1)}, u32[]{:S(2)}, u32[]{:S(2)}) collective-permute-start(bf16[2,64,512]{2,1,0:T(8,128)(2,1)S(1)} %get-tuple-element.41), channel_id=1, source_target_pairs={{1,0},{2,1},{3,2},{5,4},{6,5},{7,6},{9,8},{10,9},{11,10},{13,12},{... | collective-permute-start | bytes 393224 | tf_op jit(solution)/shard_map/ppermute | solution.py:29
